TPU v7x, 256 devices: a whole 4x4x8 slice. The times are simulated.
256 devices in a mesh: gx: 32 (over z, x), gy: 8 (over y, core).
Axes of the slice: x: 4, y: 4, z: 8, core: 2. Of those that a mesh axis runs over, the one named last changes fastest.
Arguments:
- mode_fields: float32 [32, 2048, 2048], P(None, 'gx', 'gy'), may hold values from -60 to 60, as said below
- conductance: float32 [2048, 2048], P('gx', 'gy'), may hold values from 0.5 to 2
- potential: float32 [2048, 2048], P('gx', 'gy'), may hold values from 0.25 to 4
Outputs:
- basis_field: float32 [128, 2048, 2048], P(None, 'gx', 'gy')
- scaled_factor: float32 [128, 128], replicated
Inputs may be any that keep to these rules, and one draw needn't show every extreme that they name: `mode_fields`: Real-valued mode amplitudes.
All inputs are finite; a program needn't handle non-finite values.
Results may differ from a plain program's by a relative error of at most 0.0003.
Values sent between devices are 32-bit elements; how exact they have to be, the bound alone decides.
No kernel may reach another device: no remote copies, remote signals or barrier semaphores. Data moves between devices by JAX's collectives and lax.ppermute only.
A program may use at most 64 MiB of HBM per device.

v0:
```python
import jax
import jax.numpy as jnp
from jax import lax
from jax.sharding import PartitionSpec as P


def padded_2(value, sides, width):
    for axis, dim in sides:
        peers, length = (lax.axis_size(axis), value.shape[dim])
        up = [(i, (i + 1) % peers) for i in range(peers - 1)]
        down = [(j, i) for i, j in up]
        last = lax.slice_in_dim(value, length - width, length, axis=dim)
        first = lax.slice_in_dim(value, 0, width, axis=dim)
        before = lax.ppermute(last, axis, up)
        after = lax.ppermute(first, axis, down)
        value = jnp.concatenate([before, value, after], axis=dim)
    return value


def build_columns(fields, conduct, potential):
    center = fields[:, 1:-1, 1:-1]
    k_mid = conduct[1:-1, 1:-1]
    x_plus = 0.5 * (k_mid + conduct[2:, 1:-1])
    x_minus = 0.5 * (k_mid + conduct[:-2, 1:-1])
    y_plus = 0.5 * (k_mid + conduct[1:-1, 2:])
    y_minus = 0.5 * (k_mid + conduct[1:-1, :-2])
    along_x = x_plus * (center - fields[:, 2:, 1:-1]) + x_minus * (center - fields[:, :-2, 1:-1])
    along_y = y_plus * (center - fields[:, 1:-1, 2:]) + y_minus * (center - fields[:, 1:-1, :-2])
    react = potential * center
    stacked = jnp.concatenate([center, along_x, along_y, react], 0)
    return stacked.reshape(stacked.shape[0], -1)


def inner_products(matrix, cell_count):
    return jnp.dot(matrix, matrix.T, precision=lax.Precision.HIGHEST) / cell_count


def on_device(mode_fields, conductance, potential):
    modes_count = mode_fields.shape[0]
    rows_here = mode_fields.shape[1]
    cols_here = mode_fields.shape[2]
    stacked = jnp.concatenate([mode_fields, conductance[None]], 0)
    padded = padded_2(stacked, (("gx", 1), ("gy", 2)), 1)
    matrix = build_columns(padded[:modes_count], padded[modes_count], potential)
    cell_count = float(rows_here * cols_here * lax.axis_size("gx") * lax.axis_size("gy"))
    gram_total = lax.psum(inner_products(matrix, cell_count), ("gx", "gy"))
    lower_tri = jnp.linalg.cholesky(gram_total)
    basis_flat = jax.scipy.linalg.solve_triangular(lower_tri, matrix, lower=True)
    basis_field = basis_flat.reshape(basis_flat.shape[0], rows_here, cols_here)
    return (basis_field, lower_tri.T)


def solution(mesh):
    placed = (P(None, "gx", "gy"), P("gx", "gy"), P("gx", "gy"))
    return jax.shard_map(
        on_device, mesh=mesh, in_specs=placed, out_specs=(P(None, "gx", "gy"), P()), check_vma=False
    )
```

profile of v0, /device:TPU:32, one launch (start us, length us, event | category | flops | bytes accessed | tf_op | source)
XLA Modules:
  0.0 350.5 jit_solution(881422599001644900)
XLA Ops:
  7.2 0.0 all-reduce.2.cloned.1.call-start
  7.2 0.9 broadcast_in_dim.3
  8.1 5.0 %fusion.22 = (f32[32,64,256]{2,0,1:T(8,128)}, f32[33,64,256]{2,0,1:T(8,128)S(1)}, f32[32,64,256]{2,0,1:T(8,128)}) fusion(f32[32,64,256]{2,1,0:T(8,128)} %param.3, f32[64,256]{1,0:T(8,128)} %param.5), kind=kLoop, calls=%fused_computation.51 | loop fusion | flops 524287 | bytes 8454144 | tf_op args[0]
  13.1 0.9 dynamic-update-slice.4
  14.0 3.4 collective-permute-start
  17.4 4.6 %collective-permute-start.1 = (f32[33,1,256]{2,0,1:T(8,128)S(1)}, f32[33,1,256]{2,0,1:T(8,128)S(1)}, u32[]{:S(2)}, u32[]{:S(2)}) collective-permute-start(f32[33,1,256]{2,0,1:T(8,128)S(1)} %get-tuple-element.13), channel_id=1, source_target_pairs={{8,0},{16,8},{24,16},{32,24},{40,32},{48,40},{56,48},{64,56},{72,6... | collective-permute-start | bytes 101384 | tf_op jit(solution)/shard_map/ppermute | solution.py:15
  21.9 0.0 collective-permute-done
  22.0 1.6 collective-permute-done.1
  23.6 0.2 pad_maximum_fusion.1
  23.8 1.9 fusion.20
  25.7 1.8 copy.32
  27.5 1.3 collective-permute-start.3
  28.8 1.8 copy.31
  30.6 3.0 collective-permute-start.2
  33.6 0.0 collective-permute-done.3
  33.6 1.7 copy.34
  35.3 0.0 collective-permute-done.2
  35.3 1.7 copy.33
  37.0 0.0 copy-start
  37.0 0.0 copy-start.1
  37.0 0.0 copy-start.2
  37.0 1.5 pad_maximum_fusion.10
  38.5 0.1 fusion.16
  38.7 0.0 copy-done
  38.7 0.2 copy-done.1
  38.9 0.7 copy-done.2
  39.5 0.0 copy-start.3
  39.5 7.0 %fusion.9 = (f32[32,64,256]{2,0,1:T(8,128)}, f32[32,64,256]{2,0,1:T(8,128)}) fusion(f32[33,64,256]{2,0,1:T(8,128)S(1)} %dynamic-update-slice.4, f32[33,1,256]{2,0,1:T(8,128)S(1)} %collective-permute-done, f32[33,1,256]{2,0,1:T(8,128)S(1)} %collective-permute-done.1, f32[64,256]{1,0:T(8,128)S(1)} %get-tuple-element.19, f32[64,256]{1,0:T(8,128)S(1)} %get-tuple-element.17, ...), kind=kLoop, calls=%fused_computation.18 | loop fusion | flops 9437184 | bytes 8801296 | tf_op jit(solution)/shard_map/add | solution.py:27
  46.5 0.0 copy-done.3
  46.5 0.0 copy-start.4
  46.5 10.7 %fusion.12 = f32[128,128]{0,1:T(8,128)} fusion(f32[32,64,256]{2,0,1:T(8,128)} %get-tuple-element.16, f32[32,64,256]{2,0,1:T(8,128)} %get-tuple-element.9, f32[32,64,256]{2,0,1:T(8,128)} %get-tuple-element.8, f32[32,64,256]{2,0,1:T(8,128)S(1)} %copy-done.3), kind=kOutput, calls=%fused_computation.23 | convolution fusion | flops 3227533312 | bytes 8454144 | tf_op jit(solution)/shard_map/dot_general | solution.py:35
  57.2 0.0 all-reduce.2.cloned.1.call-update
  57.2 0.0 copy-done.4
  57.2 5.7 %pad_maximum_fusion = f32[128,64,256]{2,0,1:T(8,128)} fusion(f32[32,64,256]{2,0,1:T(8,128)} %get-tuple-element.16, f32[32,64,256]{2,0,1:T(8,128)} %get-tuple-element.9, f32[32,64,256]{2,0,1:T(8,128)} %get-tuple-element.8, f32[32,64,256]{2,0,1:T(8,128)S(1)} %copy-done.4), kind=kLoop, calls=%fused_computation | loop fusion | flops 6291456 | bytes 16777216 | tf_op jit(solution)/shard_map/concatenate | solution.py:30
  62.9 9.0 %copy.45 = f32[128,64,256]{0,2,1:T(8,128)} copy(f32[128,64,256]{2,0,1:T(8,128)} %pad_maximum_fusion) | data formatting | bytes 16777216 | tf_op jit(solution)/shard_map/concatenate | solution.py:30
  71.9 227.3 %all-reduce.2.cloned.1.call-done = f32[128,128]{0,1:T(8,128)} async-done(((f32[128,128]{0,1:T(8,128)}), f32[128,128]{0,1:T(8,128)}) %all-reduce.2.cloned.1.call-update) | async-done | bytes 65552 | tf_op jit(solution)/shard_map/psum | solution.py:46
  299.3 0.9 copy.44
  300.2 0.9 fusion.18
  301.0 11.7 %cholesky.16 = f32[128,128]{1,0:T(8,128)S(1)} custom-call(f32[128,128]{1,0:T(8,128)S(1)} %fusion.18), custom_call_target="Cholesky" | custom-call | tf_op jit(solution)/shard_map/jit(cholesky)/cholesky | solution.py:47
  312.8 0.6 compare_reduce_fusion
  313.4 0.7 fusion.19
  314.1 0.7 copy.48
  314.8 9.8 %custom-call.7 = f32[1,128,128]{1,2,0:T(8,128)S(1)} custom-call(f32[1,128,128]{2,1,0:T(8,128)S(1)} %get-tuple-element.22), custom_call_target="InvertDiagBlocksLowerTriangular" | custom-call | tf_op jit(solution)/shard_map/jit(_solve_triangular)/triangular_solve | solution.py:48
  324.6 10.7 %fusion = f32[128,64,256]{2,0,1:T(8,128)S(1)} fusion(f32[128,64,256]{0,2,1:T(8,128)} %copy.45, f32[1,128,128]{1,2,0:T(8,128)S(1)} %custom-call.7), kind=kOutput, calls=%fused_computation.1 | convolution fusion | flops 3221225472 | bytes 16842752 | tf_op jit(solution)/shard_map/jit(_solve_triangular)/triangular_solve | solution.py:48
  335.4 8.3 %copy.47 = f32[128,64,256]{2,1,0:T(8,128)} copy(f32[128,64,256]{2,0,1:T(8,128)S(1)} %fusion) | data formatting | bytes 16777216
  (3 shorter events, 0.1 us)
Async XLA Ops:
  7.2 292.1 %all-reduce.2.cloned.1.call-start = ((), (), s32[]{:S(2)}) async-start(), calls=%async_computation | async-start | bytes 131072 | tf_op jit(solution)/shard_map/psum | solution.py:46
  14.0 8.0 %collective-permute-start = (f32[33,1,256]{2,0,1:T(8,128)S(1)}, f32[33,1,256]{2,0,1:T(8,128)S(1)}, u32[]{:S(2)}, u32[]{:S(2)}) collective-permute-start(f32[33,1,256]{2,0,1:T(8,128)S(1)} %get-tuple-element.12), channel_id=1, source_target_pairs={{0,8},{8,16},{16,24},{24,32},{32,40},{40,48},{48,56},{56,64},{64,7... | collective-permute-start | bytes 101384 | tf_op jit(solution)/shard_map/ppermute | solution.py:14
  17.4 6.2 %collective-permute-start.1 = (f32[33,1,256]{2,0,1:T(8,128)S(1)}, f32[33,1,256]{2,0,1:T(8,128)S(1)}, u32[]{:S(2)}, u32[]{:S(2)}) collective-permute-start(f32[33,1,256]{2,0,1:T(8,128)S(1)} %get-tuple-element.13), channel_id=1, source_target_pairs={{8,0},{16,8},{24,16},{32,24},{40,32},{48,40},{56,48},{64,56},{72,6... | collective-permute-start | bytes 101384 | tf_op jit(solution)/shard_map/ppermute | solution.py:15
  27.5 6.1 %collective-permute-start.3 = (f32[33,66,1]{1,2,0:T(1,128)S(1)}, f32[33,66,1]{1,2,0:T(1,128)S(1)}, u32[]{:S(2)}, u32[]{:S(2)}) collective-permute-start(f32[33,66,1]{1,2,0:T(1,128)S(1)} %copy.32), channel_id=1, source_target_pairs={{1,0},{2,1},{3,2},{4,3},{5,4},{6,5},{7,6},{9,8},{10,9},{11,10},{12... | collective-permute-start | bytes 26144 | tf_op jit(solution)/shard_map/ppermute | solution.py:15
  30.6 4.7 %collective-permute-start.2 = (f32[33,66,1]{1,2,0:T(1,128)S(1)}, f32[33,66,1]{1,2,0:T(1,128)S(1)}, u32[]{:S(2)}, u32[]{:S(2)}) collective-permute-start(f32[33,66,1]{1,2,0:T(1,128)S(1)} %copy.31), channel_id=1, source_target_pairs={{0,1},{1,2},{2,3},{3,4},{4,5},{5,6},{6,7},{8,9},{9,10},{10,11},{11... | collective-permute-start | bytes 26144 | tf_op jit(solution)/shard_map/ppermute | solution.py:14
  37.0 1.7 copy-start
  37.0 1.9 copy-start.1
  37.0 2.6 copy-start.2
  39.5 7.0 %copy-start.3 = (f32[32,64,256]{2,0,1:T(8,128)S(1)}, f32[32,64,256]{2,0,1:T(8,128)}, u32[]{:S(2)}) copy-start(f32[32,64,256]{2,0,1:T(8,128)} %get-tuple-element.14) | copy-start | bytes 6291460
  46.5 10.7 %copy-start.4 = (f32[32,64,256]{2,0,1:T(8,128)S(1)}, f32[32,64,256]{2,0,1:T(8,128)}, u32[]{:S(2)}) copy-start(f32[32,64,256]{2,0,1:T(8,128)} %get-tuple-element.14) | copy-start | bytes 6291460
Sparse Core Ops, SparseCore 0:
  57.3 241.8 all-reduce.1
where the time goes:
time: 354 us; the launch traced here: 350 us
  waiting for transfers between devices  229 us (65%)
  other arithmetic  43.2 us (12%)
  local copies, waits for them, and re-layouts  30.4 us (9%)
  matrix products  21.4 us (6%)
  between operations  14.2 us (4%)
  starting transfers between devices  12.3 us (3%)
    psum x1, waiting for transfers between devices, on_device(): gram_total = lax.psum(inner_products(matrix, cell_count), ('gx', 'gy'))  227 us
    another operation x3, other arithmetic, on_device(): lower_tri = jnp.linalg.cholesky(gram_total)  12.4 us
    another operation x1, matrix products, on_device(): jax.scipy.linalg.solve_triangular(lower_tri, matrix, lower=True)  10.7 us
    dot_general x1, matrix products, inner_products(): jnp.dot(matrix, matrix.T, precision=lax.Precision.HIGHEST) / cell_count  10.7 us
    unnamed x13, local copies, waits for them, and re-layouts  9.88 us
    another operation x1, other arithmetic, on_device(): jax.scipy.linalg.solve_triangular(lower_tri, matrix, lower=True)  9.81 us
    concatenate x1, local copies, waits for them, and re-layouts, build_columns(): stacked = jnp.concatenate([center, along_x, along_y, react], 0)  9 us
  transfers between devices with their start and end apart: 5, of which 2 were waited for; matrix products, arithmetic and copies ran while one was open for 5% of the time, Pallas kernels for 0%

commit v1 on v0

v1 whole, which is shorter than its diff:
```python
import jax
import jax.numpy as jnp
from jax import lax
from jax.experimental import pallas as pl
from jax.experimental.pallas import tpu as pltpu
from jax.sharding import PartitionSpec as P

F32 = jnp.float32
BF16 = jnp.bfloat16
K = 32
C = 128
NB = 8


def iota(shape, dim):
    return lax.broadcasted_iota(jnp.int32, shape, dim)


def edges_kernel(rows, cols, ua_ref, ub_ref, k_ref, top_ref, bottom_ref, left_ref, right_ref):
    for ref, at in ((top_ref, 0), (bottom_ref, rows - 1)):
        ref[:K, :128] = ua_ref[pl.ds(at, K, stride=rows), :]
        ref[:K, cols - 128 :] = ub_ref[pl.ds(at, K, stride=rows), :]
        ref[K:, :] = jnp.broadcast_to(k_ref[at : at + 1, :], (8, cols))
    lane = iota((8, 128), 1)
    left = [jnp.zeros((8, 128), F32)] * (K // 8 + 1)
    right = [jnp.zeros((8, 128), F32)] * (K // 8 + 1)
    for i in range(rows):
        here = lane == i
        field_a = ua_ref[pl.ds(i, K, stride=rows), :]
        field_b = ub_ref[pl.ds(i, K, stride=rows), :]
        conduct = jnp.broadcast_to(k_ref[i : i + 1, :], (8, cols))
        for b in range(K // 8 + 1):
            if b == K // 8:
                first, last = conduct[:, :128], conduct[:, cols - 128 :]
            else:
                first, last = field_a[8 * b : 8 * b + 8], field_b[8 * b : 8 * b + 8]
            left[b] = jnp.where(here, pltpu.roll(first, i, 1) if i else first, left[b])
            right[b] = jnp.where(here, pltpu.roll(last, (i + 1) % 128, 1), right[b])
    for b in range(K // 8 + 1):
        left_ref[8 * b : 8 * b + 8, :] = left[b]
        right_ref[8 * b : 8 * b + 8, :] = right[b]


def edges(u2, conduct):
    rows, cols = conduct.shape
    whole = lambda shape: pl.BlockSpec(shape, lambda s: (0, 0))
    side = lambda t: pl.BlockSpec((K * rows, 128), lambda s: (0, t))
    sizes = [(K + 8, cols)] * 2 + [(K + 8, 128)] * 2
    return pl.pallas_call(
        lambda *refs: edges_kernel(rows, cols, *refs),
        name="edges",
        grid=(1,),
        out_shape=[jax.ShapeDtypeStruct(n, F32) for n in sizes],
        in_specs=[side(0), side(cols // 128 - 1), whole((rows, cols))],
        out_specs=[whole(n) for n in sizes],
        compiler_params=pltpu.CompilerParams(vmem_limit_bytes=16 << 20),
    )(u2, u2, conduct)


def gram_kernel(rows, cols, scale, ua_ref, ub_ref, k_ref, v_ref, up_ref, dn_ref, lf_ref, rt_ref, gram_ref, mhl_ref, acc_ref):
    step = pl.program_id(0)
    per = 8
    lane = iota((K, 128), 1)
    lane8 = iota((8, 128), 1)
    nt = cols // 128

    def field(i):
        return jnp.concatenate([r[pl.ds(i, K, stride=rows), :] for r in (ua_ref, ub_ref)], 1)

    def tiles(a):
        return [a[:, 128 * t : 128 * t + 128] for t in range(nt)]

    def shifted_left(parts, edge, lanes):
        turned = [pltpu.roll(p, 127, 1) for p in parts] + [edge]
        return [jnp.where(lanes == 127, turned[t + 1], turned[t]) for t in range(nt)]

    def shifted_right(parts, edge, lanes):
        turned = [edge] + [pltpu.roll(p, 1, 1) for p in parts]
        return [jnp.where(lanes == 0, turned[t], turned[t + 1]) for t in range(nt)]

    def spread(row):
        return jnp.broadcast_to(row[0:1, :], (K, 128))

    base = step * per
    is_first = step == 0
    is_last = step == rows // per - 1
    before = jnp.where(is_first, up_ref[...], jnp.concatenate([field(jnp.maximum(base - 1, 0)), jnp.broadcast_to(k_ref[pl.ds(jnp.maximum(base - 1, 0), 1), :], (8, cols))], 0))
    after = jnp.where(is_last, dn_ref[...], jnp.concatenate([field(jnp.minimum(base + per, rows - 1)), jnp.broadcast_to(k_ref[pl.ds(jnp.minimum(base + per, rows - 1), 1), :], (8, cols))], 0))
    u_now = field(base)
    k_now = k_ref[pl.ds(base, 1), :]
    flux_before = [
        spread(a) * (b - c)
        for a, b, c in zip(tiles(0.5 * (before[K : K + 1] + k_now)), tiles(before[:K]), tiles(u_now))
    ]
    for n in range(per):
        i = base + n
        if n < per - 1:
            u_next, k_next = field(i + 1), k_ref[pl.ds(i + 1, 1), :]
        else:
            u_next, k_next = after[:K], after[K : K + 1]
        u_t, k_t = tiles(u_now), tiles(k_now)
        flux = [
            spread(a) * (b - c) for a, b, c in zip(tiles(0.5 * (k_now + k_next)), u_t, tiles(u_next))
        ]
        left = pltpu.roll(lf_ref[...], 128 - i, 1)
        right = pltpu.roll(rt_ref[...], 127 - i, 1)
        k_right = shifted_left(k_t, right[K : K + 1], lane8[:1])
        u_right = shifted_left(u_t, right[:K], lane)
        along = [
            spread(0.5 * (a + b)) * (c - d) for a, b, c, d in zip(k_t, k_right, u_t, u_right)
        ]
        entering = spread(0.5 * (left[K : K + 1] + k_t[0])) * (left[:K] - u_t[0])
        along_before = shifted_right(along, entering, lane)
        v_t = tiles(v_ref[pl.ds(i, 1), :])
        for t in range(nt):
            m = jnp.concatenate(
                [u_t[t], flux[t] - flux_before[t], along[t] - along_before[t], spread(v_t[t]) * u_t[t]], 0
            )
            high = m.astype(BF16)
            low = (m - high.astype(F32)).astype(BF16)
            at = n * cols + 128 * t
            mhl_ref[:C, at : at + 128] = high
            mhl_ref[C:, at : at + 128] = low
        u_now, k_now, flux_before = u_next, k_next, flux
    part = lax.dot_general(
        mhl_ref[:C, :], mhl_ref[...], (((1,), (1,)), ((), ())), preferred_element_type=F32
    )

    @pl.when(is_first)
    def _():
        acc_ref[...] = part

    @pl.when(jnp.logical_not(is_first))
    def _():
        acc_ref[...] += part

    @pl.when(is_last)
    def _():
        cross = acc_ref[:, C:]
        gram_ref[...] = (acc_ref[:, :C] + (cross + cross.T)) * scale


def columns_and_gram(u2, conduct, potential, up, down, left, right, scale):
    rows, cols = conduct.shape
    whole = lambda a: pl.BlockSpec(a.shape, lambda s: (0,) * a.ndim)
    args = (u2, u2, conduct, potential, up, down, left, right)
    side = lambda t: pl.BlockSpec((u2.shape[0], 128), lambda s: (0, t))
    return pl.pallas_call(
        lambda *refs: gram_kernel(rows, cols, scale, *refs),
        name="gram",
        grid=(rows // 8,),
        out_shape=[jax.ShapeDtypeStruct((C, C), F32), jax.ShapeDtypeStruct((2 * C, rows * cols), BF16)],
        in_specs=[side(0), side(1)] + [whole(a) for a in args[2:]],
        out_specs=[pl.BlockSpec((C, C), lambda s: (0, 0)), pl.BlockSpec((2 * C, 8 * cols), lambda s: (0, s))],
        scratch_shapes=[pltpu.VMEM((C, 2 * C), F32)],
        compiler_params=pltpu.CompilerParams(vmem_limit_bytes=32 << 20, dimension_semantics=("arbitrary",)),
    )(*args)


def factor(gram):
    blocks = C // NB
    sub = iota((NB, C), 0)
    lane = iota((NB, C), 1)
    shape = (NB, C)
    a = [gram[NB * q : NB * q + NB] for q in range(blocks)]
    e = [jnp.where(lane == sub + NB * q, 1.0, 0.0).astype(F32) for q in range(blocks)]
    upper, inverse = [], []
    for p in range(blocks):
        col = lambda m, j: jnp.broadcast_to(m[:, NB * p + j : NB * p + j + 1], shape)
        row = lambda m, j: jnp.broadcast_to(m[j : j + 1, :], shape)
        cols = [col(a[p], j) for j in range(NB)]
        d = {(i, j): row(cols[j], i) for j in range(NB) for i in range(j + 1)}
        l, x = {}, {}
        for k in range(NB):
            r = lax.rsqrt(d[k, k])
            for j in range(k + 1, NB):
                l[k, j] = d[k, j] * r
            for i in range(k + 1, NB):
                for j in range(i, NB):
                    d[i, j] = d[i, j] - l[k, i] * l[k, j]
            x[k, k] = r
            for j in range(k):
                s = l[j, k] * x[j, j]
                for m in range(j + 1, k):
                    s = s + l[m, k] * x[m, j]
                x[k, j] = -(s * r)

        def combine(parts):
            out = []
            for k in range(NB):
                s = x[k, 0] * parts[0]
                for j in range(1, k + 1):
                    s = s + x[k, j] * parts[j]
                out.append(s)
            return out

        ra = combine([row(a[p], j) for j in range(NB)])
        re = combine([row(e[p], j) for j in range(NB)])
        ua, ue = ra[0], re[0]
        for k in range(1, NB):
            ua = jnp.where(sub == k, ra[k], ua)
            ue = jnp.where(sub == k, re[k], ue)
        upper.append(jnp.where(lane >= sub + NB * p, ua, 0.0))
        inverse.append(ue)
        for q in range(p + 1, blocks):
            c = combine([col(a[q], j) for j in range(NB)])
            sa, se = c[0] * ra[0], c[0] * re[0]
            for k in range(1, NB):
                sa, se = sa + c[k] * ra[k], se + c[k] * re[k]
            a[q], e[q] = a[q] - sa, e[q] - se
    return upper, inverse


def finish_kernel(rows, cols, gram_ref, mhl_ref, out_ref, upper_ref, m_buf, o_buf, x_ref, in_sem, out_sem):
    groups = rows // 8
    wide = 8 * cols
    sides = cols // 128

    def arrive(g):
        span = pl.ds(pl.multiple_of(g * wide, wide), wide)
        return pltpu.make_async_copy(mhl_ref.at[:, span], m_buf.at[:, span], in_sem.at[g])

    def leave(g, t):
        place = out_ref.at[:, pl.ds(pl.multiple_of(g * 8, 8), 8), 128 * t : 128 * t + 128]
        return pltpu.make_async_copy(o_buf.at[g, t].reshape(C, 8, 128), place, out_sem.at[g, t])

    for g in range(groups):
        arrive(g).start()
    upper, inverse = factor(gram_ref[...])
    for p in range(C // NB):
        upper_ref[NB * p : NB * p + NB, :] = upper[p]
    x = jnp.concatenate(inverse, 0)
    high = x.astype(BF16)
    x_ref[:C, :C] = high
    x_ref[:C, C:] = high
    x_ref[C:, :C] = (x - high.astype(F32)).astype(BF16)

    @pl.loop(0, groups)
    def _(g):
        arrive(g).wait()
        for n in range(8):
            m = m_buf[:, pl.ds(pl.multiple_of(g * wide + n * cols, cols), cols)]
            b = jnp.dot(x_ref[:C, :], m, preferred_element_type=F32)
            b = b + jnp.dot(x_ref[C:, :C], m[:C], preferred_element_type=F32)
            for t in range(sides):
                o_buf[g, t, pl.ds(n, C, stride=8), :] = b[:, 128 * t : 128 * t + 128]
        for t in range(sides):
            leave(g, t).start()

    for g in range(groups):
        for t in range(sides):
            leave(g, t).wait()


def finish(gram, mhl, rows, cols):
    full = pl.BlockSpec(memory_space=pltpu.VMEM)
    far = pl.BlockSpec(memory_space=pl.ANY)
    groups = rows // 8
    return pl.pallas_call(
        lambda *refs: finish_kernel(rows, cols, *refs),
        name="finish",
        out_shape=[jax.ShapeDtypeStruct((C, rows, cols), F32), jax.ShapeDtypeStruct((C, C), F32)],
        in_specs=[full, far],
        out_specs=[far, full],
        scratch_shapes=[
            pltpu.VMEM((2 * C, rows * cols), BF16),
            pltpu.VMEM((groups, cols // 128, C * 8, 128), F32),
            pltpu.VMEM((2 * C, 2 * C), BF16),
            pltpu.SemaphoreType.DMA((groups,)),
            pltpu.SemaphoreType.DMA((groups, cols // 128)),
        ],
        compiler_params=pltpu.CompilerParams(vmem_limit_bytes=40 << 20),
    )(gram, mhl)


def butterfly_sum(value):
    rounds = (("gy", 1), ("gy", 2), ("gy", 6), ("gx", 1), ("gx", 3), ("gx", 4), ("gx", 8), ("gx", 28))
    for axis, flip in rounds:
        pairs = [(i, i ^ flip) for i in range(lax.axis_size(axis))]
        value = value + lax.ppermute(value, axis, pairs)
    return value


def on_device(mode_fields, conductance, potential):
    fields, rows, cols = mode_fields.shape
    u2 = mode_fields.reshape(fields * rows, cols)
    top, bottom, left, right = edges(u2, conductance)

    def send(value, axis, forward):
        peers = lax.axis_size(axis)
        up = [(i, i + 1) for i in range(peers - 1)]
        return lax.ppermute(value, axis, up if forward else [(j, i) for i, j in up])

    from_up = send(bottom, "gx", True)
    from_down = send(top, "gx", False)
    from_left = send(right, "gy", True)
    from_right = send(left, "gy", False)
    cells = rows * cols * lax.axis_size("gx") * lax.axis_size("gy")
    gram, mhl = columns_and_gram(u2, conductance, potential, from_up, from_down, from_left, from_right, 1.0 / cells)
    basis_field, scaled_factor = finish(butterfly_sum(gram), mhl, rows, cols)
    return (basis_field, scaled_factor)


def solution(mesh):
    placed = (P(None, "gx", "gy"), P("gx", "gy"), P("gx", "gy"))
    return jax.shard_map(
        on_device, mesh=mesh, in_specs=placed, out_specs=(P(None, "gx", "gy"), P()), check_vma=False
    )
```

time: 354 us -> 85.1 us (0.24)
  waiting for transfers between devices: 229 us -> 29.4 us
  other arithmetic: 43.2 us -> 0.07 us
  local copies, waits for them, and re-layouts: 30.4 us -> 5.69 us
  Pallas kernels: 0 us -> 22.2 us
  matrix products: 21.4 us -> 0 us
  starting transfers between devices: 12.3 us -> 26.5 us
  between operations: 14.2 us -> 0.91 us
    psum x1 -> x0, waiting for transfers between devices: 227 us -> none  [on_device(): gram_total = lax.psum(inner_products(matrix, cell_count), ('gx', 'gy'))]
    ppermute x4 -> x12, waiting for transfers between devices: 1.66 us -> 29.4 us  [the longest x8 25.8 us: butterfly_sum(): value = value + lax.ppermute(value, axis, pairs)]
    another operation x4 -> x0, other arithmetic: 22.2 us -> none  [the longest x3 12.4 us: on_device(): lower_tri = jnp.linalg.cholesky(gram_total)]
    pallas_call x0 -> x3, Pallas kernels: none -> 22.2 us  [the longest x1 11.5 us: finish(): pl.pallas_call(lambda *refs: finish_kernel(rows, cols, *refs), name='fini...]
    ppermute x4 -> x12, starting transfers between devices: 12.3 us -> 26.5 us  [the longest x8 16 us: butterfly_sum(): value = value + lax.ppermute(value, axis, pairs)]
    another operation x1 -> x0, matrix products: 10.7 us -> none  [on_device(): jax.scipy.linalg.solve_triangular(lower_tri, matrix, lower=True)]
    dot_general x1 -> x0, matrix products: 10.7 us -> none  [inner_products(): jnp.dot(matrix, matrix.T, precision=lax.Precision.HIGHEST) / cell_count]
    concatenate x2 -> x0, local copies, waits for them, and re-layouts: 9.87 us -> none  [the longest x1 9 us: build_columns(): stacked = jnp.concatenate([center, along_x, along_y, react], 0)]
  transfers between devices with their start and end apart: 5 -> 12, of which waited for: 2 -> 9; matrix products, arithmetic and copies ran while one was open for 5% -> 0% of each run, Pallas kernels for 0% -> 0%
where the time goes in v1:
time: 85.1 us; the launch traced here: 84.7 us
  waiting for transfers between devices  29.4 us (35%)
  starting transfers between devices  26.5 us (31%)
  Pallas kernels  22.2 us (26%)
  local copies, waits for them, and re-layouts  5.69 us (7%)
  between operations  0.91 us (1%)
    ppermute x8, waiting for transfers between devices, butterfly_sum(): value = value + lax.ppermute(value, axis, pairs)  25.8 us
    ppermute x8, starting transfers between devices, butterfly_sum(): value = value + lax.ppermute(value, axis, pairs)  16 us
    pallas_call x1, Pallas kernels, finish(): pl.pallas_call(lambda *refs: finish_kernel(rows, cols, *refs), name='fini...  11.5 us
    ppermute x4, starting transfers between devices, send(): return lax.ppermute(value, axis, up if forward else [(j, i) for i, j in up])  10.5 us
    pallas_call x1, Pallas kernels, columns_and_gram(): pl.pallas_call(lambda *refs: gram_kernel(rows, cols, scale, *refs), name=...  8.61 us
    unnamed x10, local copies, waits for them, and re-layouts  5.69 us
    ppermute x4, waiting for transfers between devices, send(): return lax.ppermute(value, axis, up if forward else [(j, i) for i, j in up])  3.59 us
    pallas_call x1, Pallas kernels, edges(): pl.pallas_call(lambda *refs: edges_kernel(rows, cols, *refs), name='edges...  2.1 us
  transfers between devices with their start and end apart: 12, of which 9 were waited for; matrix products, arithmetic and copies ran while one was open for 0% of the time, Pallas kernels for 0%

profile of v1, /device:TPU:32, one launch (start us, length us, event | category | flops | bytes accessed | tf_op | source)
XLA Modules:
  0.0 84.7 jit_solution(8487514062734292961)
XLA Ops:
  0.6 0.0 copy-start
  0.6 1.6 %copy-done = f32[32,64,256]{2,1,0:T(8,128)S(1)} copy-done((f32[32,64,256]{2,1,0:T(8,128)S(1)}, f32[32,64,256]{2,1,0:T(8,128)}, u32[]{:S(2)}) %copy-start) | copy-done | bytes 2097176
  2.2 0.0 copy-start.2
  2.2 0.8 copy-done.2
  3.1 2.1 %edges.1 = (f32[40,256]{1,0:T(8,128)S(1)}, f32[40,256]{1,0:T(8,128)S(1)}, f32[40,128]{1,0:T(8,128)S(1)}, f32[40,128]{1,0:T(8,128)S(1)}) custom-call(f32[2048,256]{1,0:T(8,128)S(1)} %bitcast.1, f32[2048,256]{1,0:T(8,128)S(1)} %bitcast.2, f32[64,256]{1,0:T(8,128)S(1)} %copy-done.2), custom_call_target="tpu_custom_call" | custom-call | tf_op jit(solution)/shard_map/edges/pallas_call | solution.py:49
  5.2 3.4 %collective-permute-start = (f32[40,256]{1,0:T(8,128)S(1)}, f32[40,256]{1,0:T(8,128)S(1)}, u32[]{:S(2)}, u32[]{:S(2)}) collective-permute-start(f32[40,256]{1,0:T(8,128)S(1)} %get-tuple-element.8), channel_id=1, source_target_pairs={{0,8},{8,16},{16,24},{24,32},{32,40},{40,48},{48,56},{56,64},{64,7... | collective-permute-start | bytes 122888 | tf_op jit(solution)/shard_map/ppermute | solution.py:292
  8.6 4.6 %collective-permute-start.1 = (f32[40,256]{1,0:T(8,128)S(1)}, f32[40,256]{1,0:T(8,128)S(1)}, u32[]{:S(2)}, u32[]{:S(2)}) collective-permute-start(f32[40,256]{1,0:T(8,128)S(1)} %get-tuple-element.9), channel_id=1, source_target_pairs={{8,0},{16,8},{24,16},{32,24},{40,32},{48,40},{56,48},{64,56},{72,6... | collective-permute-start | bytes 122888 | tf_op jit(solution)/shard_map/ppermute | solution.py:292
  13.1 1.3 %collective-permute-start.2 = (f32[40,128]{1,0:T(8,128)S(1)}, f32[40,128]{1,0:T(8,128)S(1)}, u32[]{:S(2)}, u32[]{:S(2)}) collective-permute-start(f32[40,128]{1,0:T(8,128)S(1)} %get-tuple-element.10), channel_id=1, source_target_pairs={{0,1},{1,2},{2,3},{3,4},{4,5},{5,6},{6,7},{8,9},{9,10},{10,11},{11... | collective-permute-start | bytes 61448 | tf_op jit(solution)/shard_map/ppermute | solution.py:292
  14.4 1.3 %collective-permute-start.3 = (f32[40,128]{1,0:T(8,128)S(1)}, f32[40,128]{1,0:T(8,128)S(1)}, u32[]{:S(2)}, u32[]{:S(2)}) collective-permute-start(f32[40,128]{1,0:T(8,128)S(1)} %get-tuple-element.11), channel_id=1, source_target_pairs={{1,0},{2,1},{3,2},{4,3},{5,4},{6,5},{7,6},{9,8},{10,9},{11,10},{12... | collective-permute-start | bytes 61448 | tf_op jit(solution)/shard_map/ppermute | solution.py:292
  15.7 0.0 collective-permute-done.2.refs_6_
  15.7 3.6 %collective-permute-done.3.refs_7_ = f32[40,128]{1,0:T(8,128)S(1)} collective-permute-done((f32[40,128]{1,0:T(8,128)S(1)}, f32[40,128]{1,0:T(8,128)S(1)}, u32[]{:S(2)}, u32[]{:S(2)}) %collective-permute-start.3) | collective-permute-done | bytes 20512 | tf_op jit(solution)/shard_map/ppermute | solution.py:292
  19.3 0.0 collective-permute-done.refs_4_
  19.3 0.0 collective-permute-done.1.refs_5_
  19.3 0.0 copy-start.1
  19.3 1.6 %copy-done.1 = f32[32,64,256]{2,1,0:T(8,128)S(1)} copy-done((f32[32,64,256]{2,1,0:T(8,128)S(1)}, f32[32,64,256]{2,1,0:T(8,128)}, u32[]{:S(2)}) %copy-start.1) | copy-done | bytes 2097176
  20.9 0.0 copy-start.3
  20.9 0.8 copy-done.3
  21.8 0.0 copy-start.4
  21.8 0.8 copy-done.4
  22.6 8.6 %gram.1 = (f32[128,128]{1,0:T(8,128)S(1)}, bf16[256,16384]{1,0:T(8,128)(2,1)S(1)}) custom-call(f32[2048,256]{1,0:T(8,128)S(1)} %bitcast.3, f32[2048,256]{1,0:T(8,128)S(1)} %bitcast.4, f32[64,256]{1,0:T(8,128)S(1)} %copy-done.3, f32[64,256]{1,0:T(8,128)S(1)} %copy-done.4, f32[40,256]{1,0:T(8,128)S(1)} %collective-permute-done.refs_4_, ...), custom_call_target="tpu_custom_call" | custom-call | tf_op jit(solution)/shard_map/gram/pallas_call | solution.py:148
  31.2 2.6 %collective-permute-start.4 = (f32[128,128]{1,0:T(8,128)S(1)}, f32[128,128]{1,0:T(8,128)S(1)}, u32[]{:S(2)}, u32[]{:S(2)}) collective-permute-start(f32[128,128]{1,0:T(8,128)S(1)} %get-tuple-element.12), channel_id=1, source_target_pairs={{0,1},{1,0},{2,3},{3,2},{4,5},{5,4},{6,7},{7,6},{8,9},{9,8},{10,11... | collective-permute-start | bytes 196616 | tf_op jit(solution)/shard_map/ppermute | solution.py:280
  33.8 0.9 %collective-permute-done.4 = f32[128,128]{1,0:T(8,128)S(1)} collective-permute-done((f32[128,128]{1,0:T(8,128)S(1)}, f32[128,128]{1,0:T(8,128)S(1)}, u32[]{:S(2)}, u32[]{:S(2)}) %collective-permute-start.4) | collective-permute-done | bytes 65568 | tf_op jit(solution)/shard_map/ppermute | solution.py:280
  34.7 1.7 %collective-permute-start.5 = (f32[128,128]{1,0:T(8,128)S(1)}, f32[128,128]{1,0:T(8,128)S(1)}, u32[]{:S(2)}, u32[]{:S(2)}) collective-permute-start(f32[128,128]{1,0:T(8,128)S(1)} %add.24), channel_id=1, source_target_pairs={{0,2},{1,3},{2,0},{3,1},{4,6},{5,7},{6,4},{7,5},{8,10},{9,11},{10,... | collective-permute-start | bytes 196616 | tf_op jit(solution)/shard_map/ppermute | solution.py:280
  36.4 2.8 %collective-permute-done.5 = f32[128,128]{1,0:T(8,128)S(1)} collective-permute-done((f32[128,128]{1,0:T(8,128)S(1)}, f32[128,128]{1,0:T(8,128)S(1)}, u32[]{:S(2)}, u32[]{:S(2)}) %collective-permute-start.5) | collective-permute-done | bytes 65568 | tf_op jit(solution)/shard_map/ppermute | solution.py:280
  39.2 1.8 %collective-permute-start.6 = (f32[128,128]{1,0:T(8,128)S(1)}, f32[128,128]{1,0:T(8,128)S(1)}, u32[]{:S(2)}, u32[]{:S(2)}) collective-permute-start(f32[128,128]{1,0:T(8,128)S(1)} %add.25), channel_id=1, source_target_pairs={{0,6},{1,7},{2,4},{3,5},{4,2},{5,3},{6,0},{7,1},{8,14},{9,15},{10,... | collective-permute-start | bytes 196616 | tf_op jit(solution)/shard_map/ppermute | solution.py:280
  41.0 3.8 %collective-permute-done.6 = f32[128,128]{1,0:T(8,128)S(1)} collective-permute-done((f32[128,128]{1,0:T(8,128)S(1)}, f32[128,128]{1,0:T(8,128)S(1)}, u32[]{:S(2)}, u32[]{:S(2)}) %collective-permute-start.6) | collective-permute-done | bytes 65568 | tf_op jit(solution)/shard_map/ppermute | solution.py:280
  44.8 0.1 collective-permute-start.7
  44.9 4.3 %collective-permute-done.7 = f32[128,128]{1,0:T(8,128)S(1)} collective-permute-done((f32[128,128]{1,0:T(8,128)S(1)}, f32[128,128]{1,0:T(8,128)S(1)}, u32[]{:S(2)}, u32[]{:S(2)}) %collective-permute-start.7) | collective-permute-done | bytes 65568 | tf_op jit(solution)/shard_map/ppermute | solution.py:280
  49.1 0.7 collective-permute-start.8
  49.9 4.8 %collective-permute-done.8 = f32[128,128]{1,0:T(8,128)S(1)} collective-permute-done((f32[128,128]{1,0:T(8,128)S(1)}, f32[128,128]{1,0:T(8,128)S(1)}, u32[]{:S(2)}, u32[]{:S(2)}) %collective-permute-start.8) | collective-permute-done | bytes 65568 | tf_op jit(solution)/shard_map/ppermute | solution.py:280
  54.7 0.1 collective-permute-start.9
  54.8 4.8 %collective-permute-done.9 = f32[128,128]{1,0:T(8,128)S(1)} collective-permute-done((f32[128,128]{1,0:T(8,128)S(1)}, f32[128,128]{1,0:T(8,128)S(1)}, u32[]{:S(2)}, u32[]{:S(2)}) %collective-permute-start.9) | collective-permute-done | bytes 65568 | tf_op jit(solution)/shard_map/ppermute | solution.py:280
  59.6 3.3 %collective-permute-start.10 = (f32[128,128]{1,0:T(8,128)S(1)}, f32[128,128]{1,0:T(8,128)S(1)}, u32[]{:S(2)}, u32[]{:S(2)}) collective-permute-start(f32[128,128]{1,0:T(8,128)S(1)} %add.29), channel_id=1, source_target_pairs={{0,64},{8,72},{16,80},{24,88},{32,96},{40,104},{48,112},{56,120},{... | collective-permute-start | bytes 196616 | tf_op jit(solution)/shard_map/ppermute | solution.py:280
  62.9 2.2 %collective-permute-done.10 = f32[128,128]{1,0:T(8,128)S(1)} collective-permute-done((f32[128,128]{1,0:T(8,128)S(1)}, f32[128,128]{1,0:T(8,128)S(1)}, u32[]{:S(2)}, u32[]{:S(2)}) %collective-permute-start.10) | collective-permute-done | bytes 65568 | tf_op jit(solution)/shard_map/ppermute | solution.py:280
  65.2 5.7 %collective-permute-start.11 = (f32[128,128]{1,0:T(8,128)S(1)}, f32[128,128]{1,0:T(8,128)S(1)}, u32[]{:S(2)}, u32[]{:S(2)}) collective-permute-start(f32[128,128]{1,0:T(8,128)S(1)} %add.30), channel_id=1, source_target_pairs={{0,224},{8,232},{16,240},{24,248},{32,192},{40,200},{48,208},{56,2... | collective-permute-start | bytes 196616 | tf_op jit(solution)/shard_map/ppermute | solution.py:280
  70.8 2.3 %collective-permute-done.11 = f32[128,128]{1,0:T(8,128)S(1)} collective-permute-done((f32[128,128]{1,0:T(8,128)S(1)}, f32[128,128]{1,0:T(8,128)S(1)}, u32[]{:S(2)}, u32[]{:S(2)}) %collective-permute-start.11) | collective-permute-done | bytes 65568 | tf_op jit(solution)/shard_map/ppermute | solution.py:280
  73.1 11.5 %finish.1 = (f32[128,64,256]{2,1,0:T(8,128)}, f32[128,128]{1,0:T(8,128)}) custom-call(f32[128,128]{1,0:T(8,128)S(1)} %add.31.refs_0_, bf16[256,16384]{1,0:T(8,128)(2,1)S(1)} %get-tuple-element.13.refs_1_), custom_call_target="tpu_custom_call" | custom-call | tf_op jit(solution)/shard_map/finish/pallas_call | solution.py:259
  (8 shorter events, 0.1 us)
Async XLA Ops:
  0.6 1.6 %copy-start = (f32[32,64,256]{2,1,0:T(8,128)S(1)}, f32[32,64,256]{2,1,0:T(8,128)}, u32[]{:S(2)}) copy-start(f32[32,64,256]{2,1,0:T(8,128)} %param.3) | copy-start | bytes 6291460
  2.2 0.8 copy-start.2
  5.2 14.2 %collective-permute-start = (f32[40,256]{1,0:T(8,128)S(1)}, f32[40,256]{1,0:T(8,128)S(1)}, u32[]{:S(2)}, u32[]{:S(2)}) collective-permute-start(f32[40,256]{1,0:T(8,128)S(1)} %get-tuple-element.8), channel_id=1, source_target_pairs={{0,8},{8,16},{16,24},{24,32},{32,40},{40,48},{48,56},{56,64},{64,7... | collective-permute-start | bytes 122888 | tf_op jit(solution)/shard_map/ppermute | solution.py:292
  8.6 10.8 %collective-permute-start.1 = (f32[40,256]{1,0:T(8,128)S(1)}, f32[40,256]{1,0:T(8,128)S(1)}, u32[]{:S(2)}, u32[]{:S(2)}) collective-permute-start(f32[40,256]{1,0:T(8,128)S(1)} %get-tuple-element.9), channel_id=1, source_target_pairs={{8,0},{16,8},{24,16},{32,24},{40,32},{48,40},{56,48},{64,56},{72,6... | collective-permute-start | bytes 122888 | tf_op jit(solution)/shard_map/ppermute | solution.py:292
  13.1 2.6 %collective-permute-start.2 = (f32[40,128]{1,0:T(8,128)S(1)}, f32[40,128]{1,0:T(8,128)S(1)}, u32[]{:S(2)}, u32[]{:S(2)}) collective-permute-start(f32[40,128]{1,0:T(8,128)S(1)} %get-tuple-element.10), channel_id=1, source_target_pairs={{0,1},{1,2},{2,3},{3,4},{4,5},{5,6},{6,7},{8,9},{9,10},{10,11},{11... | collective-permute-start | bytes 61448 | tf_op jit(solution)/shard_map/ppermute | solution.py:292
  14.4 4.9 %collective-permute-start.3 = (f32[40,128]{1,0:T(8,128)S(1)}, f32[40,128]{1,0:T(8,128)S(1)}, u32[]{:S(2)}, u32[]{:S(2)}) collective-permute-start(f32[40,128]{1,0:T(8,128)S(1)} %get-tuple-element.11), channel_id=1, source_target_pairs={{1,0},{2,1},{3,2},{4,3},{5,4},{6,5},{7,6},{9,8},{10,9},{11,10},{12... | collective-permute-start | bytes 61448 | tf_op jit(solution)/shard_map/ppermute | solution.py:292
  19.3 1.6 %copy-start.1 = (f32[32,64,256]{2,1,0:T(8,128)S(1)}, f32[32,64,256]{2,1,0:T(8,128)}, u32[]{:S(2)}) copy-start(f32[32,64,256]{2,1,0:T(8,128)} %param.3) | copy-start | bytes 6291460
  20.9 0.8 copy-start.3
  21.8 0.8 copy-start.4
  31.2 3.5 %collective-permute-start.4 = (f32[128,128]{1,0:T(8,128)S(1)}, f32[128,128]{1,0:T(8,128)S(1)}, u32[]{:S(2)}, u32[]{:S(2)}) collective-permute-start(f32[128,128]{1,0:T(8,128)S(1)} %get-tuple-element.12), channel_id=1, source_target_pairs={{0,1},{1,0},{2,3},{3,2},{4,5},{5,4},{6,7},{7,6},{8,9},{9,8},{10,11... | collective-permute-start | bytes 196616 | tf_op jit(solution)/shard_map/ppermute | solution.py:280
  34.7 4.4 %collective-permute-start.5 = (f32[128,128]{1,0:T(8,128)S(1)}, f32[128,128]{1,0:T(8,128)S(1)}, u32[]{:S(2)}, u32[]{:S(2)}) collective-permute-start(f32[128,128]{1,0:T(8,128)S(1)} %add.24), channel_id=1, source_target_pairs={{0,2},{1,3},{2,0},{3,1},{4,6},{5,7},{6,4},{7,5},{8,10},{9,11},{10,... | collective-permute-start | bytes 196616 | tf_op jit(solution)/shard_map/ppermute | solution.py:280
  39.2 5.6 %collective-permute-start.6 = (f32[128,128]{1,0:T(8,128)S(1)}, f32[128,128]{1,0:T(8,128)S(1)}, u32[]{:S(2)}, u32[]{:S(2)}) collective-permute-start(f32[128,128]{1,0:T(8,128)S(1)} %add.25), channel_id=1, source_target_pairs={{0,6},{1,7},{2,4},{3,5},{4,2},{5,3},{6,0},{7,1},{8,14},{9,15},{10,... | collective-permute-start | bytes 196616 | tf_op jit(solution)/shard_map/ppermute | solution.py:280
  44.8 4.4 %collective-permute-start.7 = (f32[128,128]{1,0:T(8,128)S(1)}, f32[128,128]{1,0:T(8,128)S(1)}, u32[]{:S(2)}, u32[]{:S(2)}) collective-permute-start(f32[128,128]{1,0:T(8,128)S(1)} %add.26), channel_id=1, source_target_pairs={{0,8},{8,0},{16,24},{24,16},{32,40},{40,32},{48,56},{56,48},{64,72... | collective-permute-start | bytes 196616 | tf_op jit(solution)/shard_map/ppermute | solution.py:280
  49.1 5.6 %collective-permute-start.8 = (f32[128,128]{1,0:T(8,128)S(1)}, f32[128,128]{1,0:T(8,128)S(1)}, u32[]{:S(2)}, u32[]{:S(2)}) collective-permute-start(f32[128,128]{1,0:T(8,128)S(1)} %add.27), channel_id=1, source_target_pairs={{0,24},{8,16},{16,8},{24,0},{32,56},{40,48},{48,40},{56,32},{64,88... | collective-permute-start | bytes 196616 | tf_op jit(solution)/shard_map/ppermute | solution.py:280
  54.7 4.9 %collective-permute-start.9 = (f32[128,128]{1,0:T(8,128)S(1)}, f32[128,128]{1,0:T(8,128)S(1)}, u32[]{:S(2)}, u32[]{:S(2)}) collective-permute-start(f32[128,128]{1,0:T(8,128)S(1)} %add.28), channel_id=1, source_target_pairs={{0,32},{8,40},{16,48},{24,56},{32,0},{40,8},{48,16},{56,24},{64,96... | collective-permute-start | bytes 196616 | tf_op jit(solution)/shard_map/ppermute | solution.py:280
  59.6 5.5 %collective-permute-start.10 = (f32[128,128]{1,0:T(8,128)S(1)}, f32[128,128]{1,0:T(8,128)S(1)}, u32[]{:S(2)}, u32[]{:S(2)}) collective-permute-start(f32[128,128]{1,0:T(8,128)S(1)} %add.29), channel_id=1, source_target_pairs={{0,64},{8,72},{16,80},{24,88},{32,96},{40,104},{48,112},{56,120},{... | collective-permute-start | bytes 196616 | tf_op jit(solution)/shard_map/ppermute | solution.py:280
  65.2 7.9 %collective-permute-start.11 = (f32[128,128]{1,0:T(8,128)S(1)}, f32[128,128]{1,0:T(8,128)S(1)}, u32[]{:S(2)}, u32[]{:S(2)}) collective-permute-start(f32[128,128]{1,0:T(8,128)S(1)} %add.30), channel_id=1, source_target_pairs={{0,224},{8,232},{16,240},{24,248},{32,192},{40,200},{48,208},{56,2... | collective-permute-start | bytes 196616 | tf_op jit(solution)/shard_map/ppermute | solution.py:280

commit v2 on v1

v2 whole, which is shorter than its diff:
```python
import jax
import jax.numpy as jnp
from jax import lax
from jax.experimental import pallas as pl
from jax.experimental.pallas import tpu as pltpu
from jax.sharding import PartitionSpec as P

F32 = jnp.float32
BF16 = jnp.bfloat16
K = 32
C = 128
NB = 8


def iota(shape, dim):
    return lax.broadcasted_iota(jnp.int32, shape, dim)


def edges_kernel(
    rows, cols, u_ref, k_ref, v_ref, top_ref, bottom_ref, left_ref, right_ref, rows_ref, ko_ref, vo_ref, buf, u_sem, c_sem
):
    sides = cols // 128
    groups = rows // 8

    def arrive(g, t):
        return pltpu.make_async_copy(
            u_ref.at[:, 8 * g : 8 * g + 8, 128 * t : 128 * t + 128], buf.at[g, t].reshape(K, 8, 128), u_sem.at[g, t]
        )

    k_copy = pltpu.make_async_copy(k_ref, ko_ref, c_sem.at[0])
    v_copy = pltpu.make_async_copy(v_ref, vo_ref, c_sem.at[1])
    k_copy.start()
    for g in range(groups):
        for t in range(sides):
            arrive(g, t).start()
    v_copy.start()
    k_copy.wait()
    lane = iota((8, 128), 1)
    left = [jnp.zeros((8, 128), F32)] * (K // 8 + 1)
    right = [jnp.zeros((8, 128), F32)] * (K // 8 + 1)
    for i in range(rows):
        g, n = i // 8, i % 8
        if n == 0:
            for t in range(sides):
                arrive(g, t).wait()
        here = lane == i
        parts = [buf[g, t, pl.ds(n, K, stride=8), :] for t in range(sides)]
        for t in range(sides):
            rows_ref[K * i : K * i + K, 128 * t : 128 * t + 128] = parts[t]
        conduct = jnp.broadcast_to(ko_ref[i : i + 1, :], (8, cols))
        for ref, at in ((top_ref, 0), (bottom_ref, rows - 1)):
            if i == at:
                for t in range(sides):
                    ref[:K, 128 * t : 128 * t + 128] = parts[t]
                ref[K:, :] = conduct
        for b in range(K // 8 + 1):
            if b == K // 8:
                first, last = conduct[:, :128], conduct[:, cols - 128 :]
            else:
                first, last = parts[0][8 * b : 8 * b + 8], parts[-1][8 * b : 8 * b + 8]
            left[b] = jnp.where(here, pltpu.roll(first, i, 1) if i else first, left[b])
            right[b] = jnp.where(here, pltpu.roll(last, (i + 1) % 128, 1), right[b])
    for b in range(K // 8 + 1):
        left_ref[8 * b : 8 * b + 8, :] = left[b]
        right_ref[8 * b : 8 * b + 8, :] = right[b]
    v_copy.wait()


def edges(fields, conduct, potential):
    rows, cols = conduct.shape
    far = pl.BlockSpec(memory_space=pltpu.HBM)
    near = pl.BlockSpec(memory_space=pltpu.VMEM)
    sizes = [(K + 8, cols)] * 2 + [(K + 8, 128)] * 2 + [(K * rows, cols)] + [(rows, cols)] * 2
    return pl.pallas_call(
        lambda *refs: edges_kernel(rows, cols, *refs),
        name="edges",
        out_shape=[jax.ShapeDtypeStruct(n, F32) for n in sizes],
        in_specs=[far] * 3,
        out_specs=[near] * 7,
        scratch_shapes=[
            pltpu.VMEM((rows // 8, cols // 128, K * 8, 128), F32),
            pltpu.SemaphoreType.DMA((rows // 8, cols // 128)),
            pltpu.SemaphoreType.DMA((2,)),
        ],
        compiler_params=pltpu.CompilerParams(vmem_limit_bytes=16 << 20),
    )(*[pltpu.with_memory_space_constraint(a, pltpu.HBM) for a in (fields, conduct, potential)])


def gram_kernel(rows, cols, scale, u_ref, k_ref, v_ref, up_ref, dn_ref, lf_ref, rt_ref, gram_ref, mhl_ref, acc_ref):
    per = 8
    wide = per * cols
    lane = iota((K, 128), 1)
    lane8 = iota((8, 128), 1)
    nt = cols // 128

    def field(i):
        return u_ref[pl.ds(pl.multiple_of(i * K, K), K), :]

    def tiles(a):
        return [a[:, 128 * t : 128 * t + 128] for t in range(nt)]

    def shifted_left(parts, edge, lanes):
        turned = [pltpu.roll(p, 127, 1) for p in parts] + [edge]
        return [jnp.where(lanes == 127, turned[t + 1], turned[t]) for t in range(nt)]

    def shifted_right(parts, edge, lanes):
        turned = [edge] + [pltpu.roll(p, 1, 1) for p in parts]
        return [jnp.where(lanes == 0, turned[t], turned[t + 1]) for t in range(nt)]

    def spread(row):
        return jnp.broadcast_to(row[0:1, :], (K, 128))

    acc_ref[...] = jnp.zeros_like(acc_ref)

    @pl.loop(0, rows // per)
    def _(step):
        base = step * per
        is_first = step == 0
        is_last = step == rows // per - 1
        i_before = jnp.maximum(base - 1, 0)
        i_after = jnp.minimum(base + per, rows - 1)
        u_before = jnp.where(is_first, up_ref[:K], field(i_before))
        k_before = jnp.where(is_first, up_ref[K : K + 1], k_ref[pl.ds(i_before, 1), :])
        u_after = jnp.where(is_last, dn_ref[:K], field(i_after))
        k_after = jnp.where(is_last, dn_ref[K : K + 1], k_ref[pl.ds(i_after, 1), :])
        u_now = field(base)
        k_now = k_ref[pl.ds(base, 1), :]
        flux_before = [
            spread(a) * (b - c) for a, b, c in zip(tiles(0.5 * (k_before + k_now)), tiles(u_before), tiles(u_now))
        ]
        for n in range(per):
            i = base + n
            if n < per - 1:
                u_next, k_next = field(i + 1), k_ref[pl.ds(i + 1, 1), :]
            else:
                u_next, k_next = u_after, k_after
            u_t, k_t = tiles(u_now), tiles(k_now)
            flux = [spread(a) * (b - c) for a, b, c in zip(tiles(0.5 * (k_now + k_next)), u_t, tiles(u_next))]
            left = pltpu.roll(lf_ref[...], 128 - i, 1)
            right = pltpu.roll(rt_ref[...], 127 - i, 1)
            k_right = shifted_left(k_t, right[K : K + 1], lane8[:1])
            u_right = shifted_left(u_t, right[:K], lane)
            along = [spread(0.5 * (a + b)) * (c - d) for a, b, c, d in zip(k_t, k_right, u_t, u_right)]
            entering = spread(0.5 * (left[K : K + 1] + k_t[0])) * (left[:K] - u_t[0])
            along_before = shifted_right(along, entering, lane)
            v_t = tiles(v_ref[pl.ds(i, 1), :])
            for t in range(nt):
                m = jnp.concatenate(
                    [u_t[t], flux[t] - flux_before[t], along[t] - along_before[t], spread(v_t[t]) * u_t[t]], 0
                )
                high = m.astype(BF16)
                low = (m - high.astype(F32)).astype(BF16)
                at = pl.ds(pl.multiple_of(step * wide + n * cols + 128 * t, 128), 128)
                mhl_ref[:C, at] = high
                mhl_ref[C:, at] = low
            u_now, k_now, flux_before = u_next, k_next, flux
        span = pl.ds(pl.multiple_of(step * wide, wide), wide)
        acc_ref[...] += lax.dot_general(
            mhl_ref[:C, span], mhl_ref[:, span], (((1,), (1,)), ((), ())), preferred_element_type=F32
        )

    cross = acc_ref[:, C:]
    total = (acc_ref[:, :C] + (cross + cross.T)) * scale
    lane32 = iota((32, C), 1)
    lane16 = iota((16, C), 1)
    gram_ref[:32, :] = total[:32]
    gram_ref[32:64, :] = jnp.where(lane32 >= 32, total[32:64], pltpu.roll(total[96:], 32, 1))
    gram_ref[64:, :] = jnp.where(lane16 >= 64, total[64:80], pltpu.roll(total[80:96], 64, 1))


def unpacked(packed):
    lane32 = iota((32, C), 1)
    lane16 = iota((16, C), 1)
    middle, tail = packed[32:64], packed[64:]
    upper = jnp.concatenate(
        [
            packed[:32],
            jnp.where(lane32 >= 32, middle, 0.0),
            jnp.where(lane16 >= 64, tail, 0.0),
            jnp.where(lane16 >= 64, pltpu.roll(tail, 64, 1), 0.0),
            jnp.where(lane32 >= 96, pltpu.roll(middle, 96, 1), 0.0),
        ],
        0,
    )
    return jnp.where(iota((C, C), 1) // 32 >= iota((C, C), 0) // 32, upper, upper.T)


def columns_and_gram(u_rows, conduct, potential, up, down, left, right, scale):
    rows, cols = conduct.shape
    near = pl.BlockSpec(memory_space=pltpu.VMEM)
    args = (u_rows, conduct, potential, up, down, left, right)
    return pl.pallas_call(
        lambda *refs: gram_kernel(rows, cols, scale, *refs),
        name="gram",
        out_shape=[jax.ShapeDtypeStruct((80, C), F32), jax.ShapeDtypeStruct((2 * C, rows * cols), BF16)],
        in_specs=[near] * len(args),
        out_specs=[near] * 2,
        scratch_shapes=[pltpu.VMEM((C, 2 * C), F32)],
        compiler_params=pltpu.CompilerParams(vmem_limit_bytes=32 << 20),
    )(*args)


def factor(gram):
    blocks = C // NB
    sub = iota((NB, C), 0)
    lane = iota((NB, C), 1)
    shape = (NB, C)
    a = [gram[NB * q : NB * q + NB] for q in range(blocks)]
    e = [jnp.where(lane == sub + NB * q, 1.0, 0.0).astype(F32) for q in range(blocks)]
    upper, inverse = [], []
    for p in range(blocks):
        col = lambda m, j: jnp.broadcast_to(m[:, NB * p + j : NB * p + j + 1], shape)
        row = lambda m, j: jnp.broadcast_to(m[j : j + 1, :], shape)
        cols = [col(a[p], j) for j in range(NB)]
        d = {(i, j): row(cols[j], i) for j in range(NB) for i in range(j + 1)}
        l, x = {}, {}
        for k in range(NB):
            r = lax.rsqrt(d[k, k])
            for j in range(k + 1, NB):
                l[k, j] = d[k, j] * r
            for i in range(k + 1, NB):
                for j in range(i, NB):
                    d[i, j] = d[i, j] - l[k, i] * l[k, j]
            x[k, k] = r
            for j in range(k):
                s = l[j, k] * x[j, j]
                for m in range(j + 1, k):
                    s = s + l[m, k] * x[m, j]
                x[k, j] = -(s * r)

        def combine(parts):
            out = []
            for k in range(NB):
                s = x[k, 0] * parts[0]
                for j in range(1, k + 1):
                    s = s + x[k, j] * parts[j]
                out.append(s)
            return out

        ra = combine([row(a[p], j) for j in range(NB)])
        re = combine([row(e[p], j) for j in range(NB)])
        ua, ue = ra[0], re[0]
        for k in range(1, NB):
            ua = jnp.where(sub == k, ra[k], ua)
            ue = jnp.where(sub == k, re[k], ue)
        upper.append(jnp.where(lane >= sub + NB * p, ua, 0.0))
        inverse.append(ue)
        for q in range(p + 1, blocks):
            c = combine([col(a[q], j) for j in range(NB)])
            sa, se = c[0] * ra[0], c[0] * re[0]
            for k in range(1, NB):
                sa, se = sa + c[k] * ra[k], se + c[k] * re[k]
            a[q], e[q] = a[q] - sa, e[q] - se
    return upper, inverse


def finish_kernel(rows, cols, gram_ref, mhl_ref, out_ref, upper_ref, o_buf, x_ref, out_sem):
    groups = rows // 8
    wide = 8 * cols
    sides = cols // 128

    def leave(g, t):
        place = out_ref.at[:, pl.ds(pl.multiple_of(g * 8, 8), 8), 128 * t : 128 * t + 128]
        return pltpu.make_async_copy(o_buf.at[g, t].reshape(C, 8, 128), place, out_sem.at[g, t])

    upper, inverse = factor(unpacked(gram_ref[...]))
    for p in range(C // NB):
        upper_ref[NB * p : NB * p + NB, :] = upper[p]
    x = jnp.concatenate(inverse, 0)
    high = x.astype(BF16)
    x_ref[:C, :C] = high
    x_ref[:C, C:] = high
    x_ref[C:, :C] = (x - high.astype(F32)).astype(BF16)

    @pl.loop(0, groups)
    def _(g):
        for n in range(8):
            m = mhl_ref[:, pl.ds(pl.multiple_of(g * wide + n * cols, cols), cols)]
            b = jnp.dot(x_ref[:C, :], m, preferred_element_type=F32)
            b = b + jnp.dot(x_ref[C:, :C], m[:C], preferred_element_type=F32)
            for t in range(sides):
                o_buf[g, t, pl.ds(n, C, stride=8), :] = b[:, 128 * t : 128 * t + 128]
        for t in range(sides):
            leave(g, t).start()

    for g in range(groups):
        for t in range(sides):
            leave(g, t).wait()


def finish(gram, mhl, rows, cols):
    near = pl.BlockSpec(memory_space=pltpu.VMEM)
    far = pl.BlockSpec(memory_space=pl.ANY)
    groups = rows // 8
    return pl.pallas_call(
        lambda *refs: finish_kernel(rows, cols, *refs),
        name="finish",
        out_shape=[jax.ShapeDtypeStruct((C, rows, cols), F32), jax.ShapeDtypeStruct((C, C), F32)],
        in_specs=[near, near],
        out_specs=[far, near],
        scratch_shapes=[
            pltpu.VMEM((groups, cols // 128, C * 8, 128), F32),
            pltpu.VMEM((2 * C, 2 * C), BF16),
            pltpu.SemaphoreType.DMA((groups, cols // 128)),
        ],
        compiler_params=pltpu.CompilerParams(vmem_limit_bytes=40 << 20),
    )(gram, mhl)


def exchanged(value, flips):
    across = lax.axis_size("gy")
    pairs = []
    for i in range(lax.axis_size("gx")):
        for j in range(across):
            along_x, along_y = flips[j % 2]
            pairs.append((i * across + j, (i ^ along_x) * across + (j ^ along_y)))
    return lax.ppermute(value, ("gx", "gy"), pairs)


def sum_over_devices(value):
    value = value + exchanged(value, ((0, 1), (0, 1)))
    along_x, along_y, along_z = ((1, 0), (2, 0), (3, 0)), ((0, 2), (0, 4), (0, 6)), ((4, 0), (8, 0), (12, 0))
    for group in (tuple(zip(along_x, along_y)), tuple(zip(along_y, along_x)), tuple(zip(along_z, along_z))):
        second = exchanged(value, group[1])
        first, third = exchanged(value, group[0]), exchanged(value, group[2])
        value = (value + first) + (second + third)
    return value + exchanged(value, ((28, 0), (28, 0)))


def on_device(mode_fields, conductance, potential):
    fields, rows, cols = mode_fields.shape
    top, bottom, left, right, u_rows, conduct, potent = edges(mode_fields, conductance, potential)

    def send(value, axis, forward):
        peers = lax.axis_size(axis)
        up = [(i, i + 1) for i in range(peers - 1)]
        return lax.ppermute(value, axis, up if forward else [(j, i) for i, j in up])

    from_up = send(bottom, "gx", True)
    from_down = send(top, "gx", False)
    from_left = send(right, "gy", True)
    from_right = send(left, "gy", False)
    cells = rows * cols * lax.axis_size("gx") * lax.axis_size("gy")
    gram, mhl = columns_and_gram(u_rows, conduct, potent, from_up, from_down, from_left, from_right, 1.0 / cells)
    basis_field, scaled_factor = finish(sum_over_devices(gram), mhl, rows, cols)
    return (basis_field, scaled_factor)


def solution(mesh):
    placed = (P(None, "gx", "gy"), P("gx", "gy"), P("gx", "gy"))
    return jax.shard_map(
        on_device, mesh=mesh, in_specs=placed, out_specs=(P(None, "gx", "gy"), P()), check_vma=False
    )
```

time: 85.1 us -> 70.9 us (0.83)
  waiting for transfers between devices: 29.4 us -> 15.4 us
  local copies, waits for them, and re-layouts: 5.69 us -> 0 us
  starting transfers between devices: 26.5 us -> 32.1 us
    ppermute x8 -> x11, waiting for transfers between devices: 25.8 us -> 11.8 us  [exchanged(): return lax.ppermute(value, ('gx', 'gy'), pairs)]
    unnamed x10 -> x0, local copies, waits for them, and re-layouts: 5.69 us -> none
    ppermute x8 -> x11, starting transfers between devices: 16 us -> 21.6 us  [exchanged(): return lax.ppermute(value, ('gx', 'gy'), pairs)]
    pallas_call x1, Pallas kernels: 11.5 us -> 10.6 us  [finish(): pl.pallas_call(lambda *refs: finish_kernel(rows, cols, *refs), name='fini...]
  transfers between devices with their start and end apart: 12 -> 15, of which waited for: 9 -> 11; matrix products, arithmetic and copies ran while one was open for 0% -> 0% of each run, Pallas kernels for 0% -> 0%
where the time goes in v2:
time: 70.9 us; the launch traced here: 69.8 us
  starting transfers between devices  32.1 us (45%)
  Pallas kernels  21.4 us (30%)
  waiting for transfers between devices  15.4 us (22%)
  between operations  0.86 us (1%)
    ppermute x11, starting transfers between devices, exchanged(): return lax.ppermute(value, ('gx', 'gy'), pairs)  21.6 us
    ppermute x11, waiting for transfers between devices, exchanged(): return lax.ppermute(value, ('gx', 'gy'), pairs)  11.8 us
    pallas_call x1, Pallas kernels, finish(): pl.pallas_call(lambda *refs: finish_kernel(rows, cols, *refs), name='fini...  10.6 us
    ppermute x4, starting transfers between devices, send(): return lax.ppermute(value, axis, up if forward else [(j, i) for i, j in up])  10.5 us
    pallas_call x1, Pallas kernels, columns_and_gram(): pl.pallas_call(lambda *refs: gram_kernel(rows, cols, scale, *refs), name=...  7.92 us
    ppermute x4, waiting for transfers between devices, send(): return lax.ppermute(value, axis, up if forward else [(j, i) for i, j in up])  3.59 us
    pallas_call x1, Pallas kernels, edges(): pl.pallas_call(lambda *refs: edges_kernel(rows, cols, *refs), name='edges...  2.92 us
  transfers between devices with their start and end apart: 15, of which 11 were waited for; matrix products, arithmetic and copies ran while one was open for 0% of the time, Pallas kernels for 0%

profile of v2, /device:TPU:32, one launch (start us, length us, event | category | flops | bytes accessed | tf_op | source)
XLA Modules:
  0.0 69.8 jit_solution(1795322603539513227)
XLA Ops:
  0.6 2.9 %edges.1 = (f32[40,256]{1,0:T(8,128)S(1)}, f32[40,256]{1,0:T(8,128)S(1)}, f32[40,128]{1,0:T(8,128)S(1)}, f32[40,128]{1,0:T(8,128)S(1)}, f32[2048,256]{1,0:T(8,12...) custom-call(f32[32,64,256]{2,1,0:T(8,128)} %refs_0_.1, f32[64,256]{1,0:T(8,128)} %refs_1_.1, f32[64,256]{1,0:T(8,128)} %refs_2_.1), custom_call_target="tpu_custom_call" | custom-call | tf_op jit(solution)/shard_map/edges/pallas_call | solution.py:74
  3.6 3.4 %collective-permute-start = (f32[40,256]{1,0:T(8,128)S(1)}, f32[40,256]{1,0:T(8,128)S(1)}, u32[]{:S(2)}, u32[]{:S(2)}) collective-permute-start(f32[40,256]{1,0:T(8,128)S(1)} %get-tuple-element.14), channel_id=1, source_target_pairs={{0,8},{8,16},{16,24},{24,32},{32,40},{40,48},{48,56},{56,64},{64,7... | collective-permute-start | bytes 122888 | tf_op jit(solution)/shard_map/ppermute | solution.py:337
  7.0 4.6 %collective-permute-start.1 = (f32[40,256]{1,0:T(8,128)S(1)}, f32[40,256]{1,0:T(8,128)S(1)}, u32[]{:S(2)}, u32[]{:S(2)}) collective-permute-start(f32[40,256]{1,0:T(8,128)S(1)} %get-tuple-element.15), channel_id=1, source_target_pairs={{8,0},{16,8},{24,16},{32,24},{40,32},{48,40},{56,48},{64,56},{72,6... | collective-permute-start | bytes 122888 | tf_op jit(solution)/shard_map/ppermute | solution.py:337
  11.5 1.3 %collective-permute-start.2 = (f32[40,128]{1,0:T(8,128)S(1)}, f32[40,128]{1,0:T(8,128)S(1)}, u32[]{:S(2)}, u32[]{:S(2)}) collective-permute-start(f32[40,128]{1,0:T(8,128)S(1)} %get-tuple-element.16), channel_id=1, source_target_pairs={{0,1},{1,2},{2,3},{3,4},{4,5},{5,6},{6,7},{8,9},{9,10},{10,11},{11... | collective-permute-start | bytes 61448 | tf_op jit(solution)/shard_map/ppermute | solution.py:337
  12.8 1.3 %collective-permute-start.3 = (f32[40,128]{1,0:T(8,128)S(1)}, f32[40,128]{1,0:T(8,128)S(1)}, u32[]{:S(2)}, u32[]{:S(2)}) collective-permute-start(f32[40,128]{1,0:T(8,128)S(1)} %get-tuple-element.17), channel_id=1, source_target_pairs={{1,0},{2,1},{3,2},{4,3},{5,4},{6,5},{7,6},{9,8},{10,9},{11,10},{12... | collective-permute-start | bytes 61448 | tf_op jit(solution)/shard_map/ppermute | solution.py:337
  14.1 0.0 collective-permute-done.2.refs_5_
  14.1 3.6 %collective-permute-done.3.refs_6_ = f32[40,128]{1,0:T(8,128)S(1)} collective-permute-done((f32[40,128]{1,0:T(8,128)S(1)}, f32[40,128]{1,0:T(8,128)S(1)}, u32[]{:S(2)}, u32[]{:S(2)}) %collective-permute-start.3) | collective-permute-done | bytes 20512 | tf_op jit(solution)/shard_map/ppermute | solution.py:337
  17.7 0.0 collective-permute-done.refs_3_
  17.7 0.0 collective-permute-done.1.refs_4_
  17.7 7.9 %gram.1 = (f32[80,128]{1,0:T(8,128)S(1)}, bf16[256,16384]{1,0:T(8,128)(2,1)S(1)}) custom-call(f32[2048,256]{1,0:T(8,128)S(1)} %get-tuple-element.11.refs_0_, f32[64,256]{1,0:T(8,128)S(1)} %get-tuple-element.12.refs_1_, f32[64,256]{1,0:T(8,128)S(1)} %get-tuple-element.13.refs_2_, f32[40,256]{1,0:T(8,128)S(1)} %collective-permute-done.refs_3_, ...), custom_call_target="tpu_custom_call" | custom-call | tf_op jit(solution)/shard_map/gram/pallas_call | solution.py:192
  25.6 2.6 %collective-permute-start.4 = (f32[80,128]{1,0:T(8,128)S(1)}, f32[80,128]{1,0:T(8,128)S(1)}, u32[]{:S(2)}, u32[]{:S(2)}) collective-permute-start(f32[80,128]{1,0:T(8,128)S(1)} %get-tuple-element.18), channel_id=1, source_target_pairs={{0,1},{1,0},{2,3},{3,2},{4,5},{5,4},{6,7},{7,6},{8,9},{9,8},{10,11... | collective-permute-start | bytes 122888 | tf_op jit(solution)/shard_map/ppermute | solution.py:317
  28.3 0.9 %collective-permute-done.4 = f32[80,128]{1,0:T(8,128)S(1)} collective-permute-done((f32[80,128]{1,0:T(8,128)S(1)}, f32[80,128]{1,0:T(8,128)S(1)}, u32[]{:S(2)}, u32[]{:S(2)}) %collective-permute-start.4) | collective-permute-done | bytes 40992 | tf_op jit(solution)/shard_map/ppermute | solution.py:317
  29.1 0.6 collective-permute-start.7
  29.8 0.8 %collective-permute-start.6 = (f32[80,128]{1,0:T(8,128)S(1)}, f32[80,128]{1,0:T(8,128)S(1)}, u32[]{:S(2)}, u32[]{:S(2)}) collective-permute-start(f32[80,128]{1,0:T(8,128)S(1)} %add.33), channel_id=1, source_target_pairs={{0,16},{1,5},{2,18},{3,7},{4,20},{5,1},{6,22},{7,3},{8,24},{9,13},... | collective-permute-start | bytes 122888 | tf_op jit(solution)/shard_map/ppermute | solution.py:317
  30.6 2.7 %collective-permute-start.5 = (f32[80,128]{1,0:T(8,128)S(1)}, f32[80,128]{1,0:T(8,128)S(1)}, u32[]{:S(2)}, u32[]{:S(2)}) collective-permute-start(f32[80,128]{1,0:T(8,128)S(1)} %add.33), channel_id=1, source_target_pairs={{0,8},{1,3},{2,10},{3,1},{4,12},{5,7},{6,14},{7,5},{8,0},{9,11},{1... | collective-permute-start | bytes 122888 | tf_op jit(solution)/shard_map/ppermute | solution.py:317
  33.2 1.1 %collective-permute-done.7 = f32[80,128]{1,0:T(8,128)S(1)} collective-permute-done((f32[80,128]{1,0:T(8,128)S(1)}, f32[80,128]{1,0:T(8,128)S(1)}, u32[]{:S(2)}, u32[]{:S(2)}) %collective-permute-start.7) | collective-permute-done | bytes 40992 | tf_op jit(solution)/shard_map/ppermute | solution.py:317
  34.3 0.9 %collective-permute-done.6 = f32[80,128]{1,0:T(8,128)S(1)} collective-permute-done((f32[80,128]{1,0:T(8,128)S(1)}, f32[80,128]{1,0:T(8,128)S(1)}, u32[]{:S(2)}, u32[]{:S(2)}) %collective-permute-start.6) | collective-permute-done | bytes 40992 | tf_op jit(solution)/shard_map/ppermute | solution.py:317
  35.3 0.4 collective-permute-done.5
  35.7 1.8 %collective-permute-start.10 = (f32[80,128]{1,0:T(8,128)S(1)}, f32[80,128]{1,0:T(8,128)S(1)}, u32[]{:S(2)}, u32[]{:S(2)}) collective-permute-start(f32[80,128]{1,0:T(8,128)S(1)} %add_add_fusion.2), channel_id=1, source_target_pairs={{0,6},{1,25},{2,4},{3,27},{4,2},{5,29},{6,0},{7,31},{8,14},{9,17},... | collective-permute-start | bytes 122888 | tf_op jit(solution)/shard_map/ppermute | solution.py:317
  37.4 2.0 %collective-permute-start.9 = (f32[80,128]{1,0:T(8,128)S(1)}, f32[80,128]{1,0:T(8,128)S(1)}, u32[]{:S(2)}, u32[]{:S(2)}) collective-permute-start(f32[80,128]{1,0:T(8,128)S(1)} %add_add_fusion.2), channel_id=1, source_target_pairs={{0,4},{1,17},{2,6},{3,19},{4,0},{5,21},{6,2},{7,23},{8,12},{9,25},... | collective-permute-start | bytes 122888 | tf_op jit(solution)/shard_map/ppermute | solution.py:317
  39.4 0.5 collective-permute-start.8
  39.8 1.1 %collective-permute-done.10 = f32[80,128]{1,0:T(8,128)S(1)} collective-permute-done((f32[80,128]{1,0:T(8,128)S(1)}, f32[80,128]{1,0:T(8,128)S(1)}, u32[]{:S(2)}, u32[]{:S(2)}) %collective-permute-start.10) | collective-permute-done | bytes 40992 | tf_op jit(solution)/shard_map/ppermute | solution.py:317
  41.0 2.0 %collective-permute-done.9 = f32[80,128]{1,0:T(8,128)S(1)} collective-permute-done((f32[80,128]{1,0:T(8,128)S(1)}, f32[80,128]{1,0:T(8,128)S(1)}, u32[]{:S(2)}, u32[]{:S(2)}) %collective-permute-start.9) | collective-permute-done | bytes 40992 | tf_op jit(solution)/shard_map/ppermute | solution.py:317
  42.9 0.4 collective-permute-done.8
  43.4 2.0 %collective-permute-start.13 = (f32[80,128]{1,0:T(8,128)S(1)}, f32[80,128]{1,0:T(8,128)S(1)}, u32[]{:S(2)}, u32[]{:S(2)}) collective-permute-start(f32[80,128]{1,0:T(8,128)S(1)} %add_add_fusion.1), channel_id=1, source_target_pairs={{0,96},{1,97},{2,98},{3,99},{4,100},{5,101},{6,102},{7,103},{8,104... | collective-permute-start | bytes 122888 | tf_op jit(solution)/shard_map/ppermute | solution.py:317
  45.4 2.1 %collective-permute-start.12 = (f32[80,128]{1,0:T(8,128)S(1)}, f32[80,128]{1,0:T(8,128)S(1)}, u32[]{:S(2)}, u32[]{:S(2)}) collective-permute-start(f32[80,128]{1,0:T(8,128)S(1)} %add_add_fusion.1), channel_id=1, source_target_pairs={{0,64},{1,65},{2,66},{3,67},{4,68},{5,69},{6,70},{7,71},{8,72},{9,... | collective-permute-start | bytes 122888 | tf_op jit(solution)/shard_map/ppermute | solution.py:317
  47.5 1.4 %collective-permute-start.11 = (f32[80,128]{1,0:T(8,128)S(1)}, f32[80,128]{1,0:T(8,128)S(1)}, u32[]{:S(2)}, u32[]{:S(2)}) collective-permute-start(f32[80,128]{1,0:T(8,128)S(1)} %add_add_fusion.1), channel_id=1, source_target_pairs={{0,32},{1,33},{2,34},{3,35},{4,36},{5,37},{6,38},{7,39},{8,40},{9,... | collective-permute-start | bytes 122888 | tf_op jit(solution)/shard_map/ppermute | solution.py:317
  48.9 0.0 collective-permute-done.13
  48.9 1.4 %collective-permute-done.12 = f32[80,128]{1,0:T(8,128)S(1)} collective-permute-done((f32[80,128]{1,0:T(8,128)S(1)}, f32[80,128]{1,0:T(8,128)S(1)}, u32[]{:S(2)}, u32[]{:S(2)}) %collective-permute-start.12) | collective-permute-done | bytes 40992 | tf_op jit(solution)/shard_map/ppermute | solution.py:317
  50.3 1.5 %collective-permute-done.11 = f32[80,128]{1,0:T(8,128)S(1)} collective-permute-done((f32[80,128]{1,0:T(8,128)S(1)}, f32[80,128]{1,0:T(8,128)S(1)}, u32[]{:S(2)}, u32[]{:S(2)}) %collective-permute-start.11) | collective-permute-done | bytes 40992 | tf_op jit(solution)/shard_map/ppermute | solution.py:317
  51.8 5.2 %collective-permute-start.14 = (f32[80,128]{1,0:T(8,128)S(1)}, f32[80,128]{1,0:T(8,128)S(1)}, u32[]{:S(2)}, u32[]{:S(2)}) collective-permute-start(f32[80,128]{1,0:T(8,128)S(1)} %add_add_fusion), channel_id=1, source_target_pairs={{0,224},{1,225},{2,226},{3,227},{4,228},{5,229},{6,230},{7,231},{8... | collective-permute-start | bytes 122888 | tf_op jit(solution)/shard_map/ppermute | solution.py:317
  57.0 2.1 %collective-permute-done.14 = f32[80,128]{1,0:T(8,128)S(1)} collective-permute-done((f32[80,128]{1,0:T(8,128)S(1)}, f32[80,128]{1,0:T(8,128)S(1)}, u32[]{:S(2)}, u32[]{:S(2)}) %collective-permute-start.14) | collective-permute-done | bytes 40992 | tf_op jit(solution)/shard_map/ppermute | solution.py:317
  59.1 10.6 %finish.1 = (f32[128,64,256]{2,1,0:T(8,128)}, f32[128,128]{1,0:T(8,128)}) custom-call(f32[80,128]{1,0:T(8,128)S(1)} %add.43.refs_0_, bf16[256,16384]{1,0:T(8,128)(2,1)S(1)} %get-tuple-element.19.refs_1_), custom_call_target="tpu_custom_call" | custom-call | tf_op jit(solution)/shard_map/finish/pallas_call | solution.py:295
  (5 shorter events, 0.1 us)
Async XLA Ops:
  3.6 14.2 %collective-permute-start = (f32[40,256]{1,0:T(8,128)S(1)}, f32[40,256]{1,0:T(8,128)S(1)}, u32[]{:S(2)}, u32[]{:S(2)}) collective-permute-start(f32[40,256]{1,0:T(8,128)S(1)} %get-tuple-element.14), channel_id=1, source_target_pairs={{0,8},{8,16},{16,24},{24,32},{32,40},{40,48},{48,56},{56,64},{64,7... | collective-permute-start | bytes 122888 | tf_op jit(solution)/shard_map/ppermute | solution.py:337
  7.0 10.8 %collective-permute-start.1 = (f32[40,256]{1,0:T(8,128)S(1)}, f32[40,256]{1,0:T(8,128)S(1)}, u32[]{:S(2)}, u32[]{:S(2)}) collective-permute-start(f32[40,256]{1,0:T(8,128)S(1)} %get-tuple-element.15), channel_id=1, source_target_pairs={{8,0},{16,8},{24,16},{32,24},{40,32},{48,40},{56,48},{64,56},{72,6... | collective-permute-start | bytes 122888 | tf_op jit(solution)/shard_map/ppermute | solution.py:337
  11.5 2.6 %collective-permute-start.2 = (f32[40,128]{1,0:T(8,128)S(1)}, f32[40,128]{1,0:T(8,128)S(1)}, u32[]{:S(2)}, u32[]{:S(2)}) collective-permute-start(f32[40,128]{1,0:T(8,128)S(1)} %get-tuple-element.16), channel_id=1, source_target_pairs={{0,1},{1,2},{2,3},{3,4},{4,5},{5,6},{6,7},{8,9},{9,10},{10,11},{11... | collective-permute-start | bytes 61448 | tf_op jit(solution)/shard_map/ppermute | solution.py:337
  12.8 4.9 %collective-permute-start.3 = (f32[40,128]{1,0:T(8,128)S(1)}, f32[40,128]{1,0:T(8,128)S(1)}, u32[]{:S(2)}, u32[]{:S(2)}) collective-permute-start(f32[40,128]{1,0:T(8,128)S(1)} %get-tuple-element.17), channel_id=1, source_target_pairs={{1,0},{2,1},{3,2},{4,3},{5,4},{6,5},{7,6},{9,8},{10,9},{11,10},{12... | collective-permute-start | bytes 61448 | tf_op jit(solution)/shard_map/ppermute | solution.py:337
  25.6 3.5 %collective-permute-start.4 = (f32[80,128]{1,0:T(8,128)S(1)}, f32[80,128]{1,0:T(8,128)S(1)}, u32[]{:S(2)}, u32[]{:S(2)}) collective-permute-start(f32[80,128]{1,0:T(8,128)S(1)} %get-tuple-element.18), channel_id=1, source_target_pairs={{0,1},{1,0},{2,3},{3,2},{4,5},{5,4},{6,7},{7,6},{8,9},{9,8},{10,11... | collective-permute-start | bytes 122888 | tf_op jit(solution)/shard_map/ppermute | solution.py:317
  29.1 5.2 %collective-permute-start.7 = (f32[80,128]{1,0:T(8,128)S(1)}, f32[80,128]{1,0:T(8,128)S(1)}, u32[]{:S(2)}, u32[]{:S(2)}) collective-permute-start(f32[80,128]{1,0:T(8,128)S(1)} %add.33), channel_id=1, source_target_pairs={{0,24},{1,7},{2,26},{3,5},{4,28},{5,3},{6,30},{7,1},{8,16},{9,15},... | collective-permute-start | bytes 122888 | tf_op jit(solution)/shard_map/ppermute | solution.py:317
  29.8 5.5 %collective-permute-start.6 = (f32[80,128]{1,0:T(8,128)S(1)}, f32[80,128]{1,0:T(8,128)S(1)}, u32[]{:S(2)}, u32[]{:S(2)}) collective-permute-start(f32[80,128]{1,0:T(8,128)S(1)} %add.33), channel_id=1, source_target_pairs={{0,16},{1,5},{2,18},{3,7},{4,20},{5,1},{6,22},{7,3},{8,24},{9,13},... | collective-permute-start | bytes 122888 | tf_op jit(solution)/shard_map/ppermute | solution.py:317
  30.6 5.1 %collective-permute-start.5 = (f32[80,128]{1,0:T(8,128)S(1)}, f32[80,128]{1,0:T(8,128)S(1)}, u32[]{:S(2)}, u32[]{:S(2)}) collective-permute-start(f32[80,128]{1,0:T(8,128)S(1)} %add.33), channel_id=1, source_target_pairs={{0,8},{1,3},{2,10},{3,1},{4,12},{5,7},{6,14},{7,5},{8,0},{9,11},{1... | collective-permute-start | bytes 122888 | tf_op jit(solution)/shard_map/ppermute | solution.py:317
  35.7 5.3 %collective-permute-start.10 = (f32[80,128]{1,0:T(8,128)S(1)}, f32[80,128]{1,0:T(8,128)S(1)}, u32[]{:S(2)}, u32[]{:S(2)}) collective-permute-start(f32[80,128]{1,0:T(8,128)S(1)} %add_add_fusion.2), channel_id=1, source_target_pairs={{0,6},{1,25},{2,4},{3,27},{4,2},{5,29},{6,0},{7,31},{8,14},{9,17},... | collective-permute-start | bytes 122888 | tf_op jit(solution)/shard_map/ppermute | solution.py:317
  37.4 5.5 %collective-permute-start.9 = (f32[80,128]{1,0:T(8,128)S(1)}, f32[80,128]{1,0:T(8,128)S(1)}, u32[]{:S(2)}, u32[]{:S(2)}) collective-permute-start(f32[80,128]{1,0:T(8,128)S(1)} %add_add_fusion.2), channel_id=1, source_target_pairs={{0,4},{1,17},{2,6},{3,19},{4,0},{5,21},{6,2},{7,23},{8,12},{9,25},... | collective-permute-start | bytes 122888 | tf_op jit(solution)/shard_map/ppermute | solution.py:317
  39.4 4.0 %collective-permute-start.8 = (f32[80,128]{1,0:T(8,128)S(1)}, f32[80,128]{1,0:T(8,128)S(1)}, u32[]{:S(2)}, u32[]{:S(2)}) collective-permute-start(f32[80,128]{1,0:T(8,128)S(1)} %add_add_fusion.2), channel_id=1, source_target_pairs={{0,2},{1,9},{2,0},{3,11},{4,6},{5,13},{6,4},{7,15},{8,10},{9,1},{1... | collective-permute-start | bytes 122888 | tf_op jit(solution)/shard_map/ppermute | solution.py:317
  43.4 5.5 %collective-permute-start.13 = (f32[80,128]{1,0:T(8,128)S(1)}, f32[80,128]{1,0:T(8,128)S(1)}, u32[]{:S(2)}, u32[]{:S(2)}) collective-permute-start(f32[80,128]{1,0:T(8,128)S(1)} %add_add_fusion.1), channel_id=1, source_target_pairs={{0,96},{1,97},{2,98},{3,99},{4,100},{5,101},{6,102},{7,103},{8,104... | collective-permute-start | bytes 122888 | tf_op jit(solution)/shard_map/ppermute | solution.py:317
  45.4 4.9 %collective-permute-start.12 = (f32[80,128]{1,0:T(8,128)S(1)}, f32[80,128]{1,0:T(8,128)S(1)}, u32[]{:S(2)}, u32[]{:S(2)}) collective-permute-start(f32[80,128]{1,0:T(8,128)S(1)} %add_add_fusion.1), channel_id=1, source_target_pairs={{0,64},{1,65},{2,66},{3,67},{4,68},{5,69},{6,70},{7,71},{8,72},{9,... | collective-permute-start | bytes 122888 | tf_op jit(solution)/shard_map/ppermute | solution.py:317
  47.5 4.2 %collective-permute-start.11 = (f32[80,128]{1,0:T(8,128)S(1)}, f32[80,128]{1,0:T(8,128)S(1)}, u32[]{:S(2)}, u32[]{:S(2)}) collective-permute-start(f32[80,128]{1,0:T(8,128)S(1)} %add_add_fusion.1), channel_id=1, source_target_pairs={{0,32},{1,33},{2,34},{3,35},{4,36},{5,37},{6,38},{7,39},{8,40},{9,... | collective-permute-start | bytes 122888 | tf_op jit(solution)/shard_map/ppermute | solution.py:317
  51.8 7.3 %collective-permute-start.14 = (f32[80,128]{1,0:T(8,128)S(1)}, f32[80,128]{1,0:T(8,128)S(1)}, u32[]{:S(2)}, u32[]{:S(2)}) collective-permute-start(f32[80,128]{1,0:T(8,128)S(1)} %add_add_fusion), channel_id=1, source_target_pairs={{0,224},{1,225},{2,226},{3,227},{4,228},{5,229},{6,230},{7,231},{8... | collective-permute-start | bytes 122888 | tf_op jit(solution)/shard_map/ppermute | solution.py:317

commit v3 on v2

--- a/solution.py
+++ b/solution.py
@@ -24,7 +24,7 @@
 
     def arrive(g, t):
         return pltpu.make_async_copy(
-            u_ref.at[:, 8 * g : 8 * g + 8, 128 * t : 128 * t + 128], buf.at[g, t].reshape(K, 8, 128), u_sem.at[g, t]
+            u_ref.at[:, pl.ds(pl.multiple_of(8 * g, 8), 8), 128 * t : 128 * t + 128], buf.at[g, t].reshape(K, 8, 128), u_sem.at[g, t]
         )
 
     k_copy = pltpu.make_async_copy(k_ref, ko_ref, c_sem.at[0])
@@ -112,7 +112,7 @@
 
     acc_ref[...] = jnp.zeros_like(acc_ref)
 
-    @pl.loop(0, rows // per)
+    @pl.loop(0, rows // per, unroll=True)
     def _(step):
         base = step * per
         is_first = step == 0
@@ -200,7 +200,7 @@
     )(*args)
 
 
-def factor(gram):
+def factor(gram, after_panel):
     blocks = C // NB
     sub = iota((NB, C), 0)
     lane = iota((NB, C), 1)
@@ -237,6 +237,15 @@
                 out.append(s)
             return out
 
+        def solved(parts):
+            out = []
+            for j in range(NB):
+                s = x[j, j] * parts[j]
+                for k in range(j + 1, NB):
+                    s = s + x[k, j] * parts[k]
+                out.append(s)
+            return out
+
         ra = combine([row(a[p], j) for j in range(NB)])
         re = combine([row(e[p], j) for j in range(NB)])
         ua, ue = ra[0], re[0]
@@ -245,47 +254,64 @@
             ue = jnp.where(sub == k, re[k], ue)
         upper.append(jnp.where(lane >= sub + NB * p, ua, 0.0))
         inverse.append(ue)
+        wa, we = solved(ra), solved(re)
         for q in range(p + 1, blocks):
-            c = combine([col(a[q], j) for j in range(NB)])
-            sa, se = c[0] * ra[0], c[0] * re[0]
+            c = [col(a[q], j) for j in range(NB)]
+            sa, se = c[0] * wa[0], c[0] * we[0]
             for k in range(1, NB):
-                sa, se = sa + c[k] * ra[k], se + c[k] * re[k]
+                sa, se = sa + c[k] * wa[k], se + c[k] * we[k]
             a[q], e[q] = a[q] - sa, e[q] - se
+        after_panel(p, inverse)
     return upper, inverse
 
 
-def finish_kernel(rows, cols, gram_ref, mhl_ref, out_ref, upper_ref, o_buf, x_ref, out_sem):
+def finish_kernel(rows, cols, gram_ref, mhl_ref, out_ref, upper_ref, o_buf, xt_ref, xb_ref, out_sem):
     groups = rows // 8
-    wide = 8 * cols
     sides = cols // 128
-
-    def leave(g, t):
-        place = out_ref.at[:, pl.ds(pl.multiple_of(g * 8, 8), 8), 128 * t : 128 * t + 128]
-        return pltpu.make_async_copy(o_buf.at[g, t].reshape(C, 8, 128), place, out_sem.at[g, t])
-
-    upper, inverse = factor(unpacked(gram_ref[...]))
-    for p in range(C // NB):
+    half = C // 2
+    panels = C // NB
+
+    def leave(g, t, part):
+        place = out_ref.at[half * part : half * part + half, pl.ds(pl.multiple_of(8 * g, 8), 8), 128 * t : 128 * t + 128]
+        source = o_buf.at[g, t, 8 * half * part : 8 * half * (part + 1)].reshape(half, 8, 128)
+        return pltpu.make_async_copy(source, place, out_sem.at[g, t, part])
+
+    def split(x):
+        high = x.astype(BF16)
+        low = (x - high.astype(F32)).astype(BF16)
+        return jnp.concatenate([jnp.concatenate([high, high], 1), jnp.concatenate([low, jnp.zeros_like(low)], 1)], 0)
+
+    def apply(g, part, left, depth):
+        for n in range(8):
+            at = pl.ds(pl.multiple_of((8 * g + n) * cols, cols), cols)
+            high, low = mhl_ref[:depth, at], mhl_ref[C : C + depth, at]
+            b = jnp.dot(left[...], jnp.concatenate([high, low], 0), preferred_element_type=F32)
+            b = b[:half] + b[half:]
+            for t in range(sides):
+                o_buf[g, t, pl.ds(8 * half * part + n, half, stride=8), :] = b[:, 128 * t : 128 * t + 128]
+        for t in range(sides):
+            leave(g, t, part).start()
+
+    top = []
+
+    def after_panel(p, inverse):
+        if p == panels // 2 - 1:
+            xt_ref[...] = split(jnp.concatenate(inverse, 0)[:, :half])
+        later = panels - panels // 2
+        if p >= panels // 2:
+            step = p - panels // 2
+            for g in range(groups * step // later, groups * (step + 1) // later):
+                apply(g, 0, xt_ref, half)
+
+    upper, inverse = factor(unpacked(gram_ref[...]), after_panel)
+    for p in range(panels):
         upper_ref[NB * p : NB * p + NB, :] = upper[p]
-    x = jnp.concatenate(inverse, 0)
-    high = x.astype(BF16)
-    x_ref[:C, :C] = high
-    x_ref[:C, C:] = high
-    x_ref[C:, :C] = (x - high.astype(F32)).astype(BF16)
-
-    @pl.loop(0, groups)
-    def _(g):
-        for n in range(8):
-            m = mhl_ref[:, pl.ds(pl.multiple_of(g * wide + n * cols, cols), cols)]
-            b = jnp.dot(x_ref[:C, :], m, preferred_element_type=F32)
-            b = b + jnp.dot(x_ref[C:, :C], m[:C], preferred_element_type=F32)
-            for t in range(sides):
-                o_buf[g, t, pl.ds(n, C, stride=8), :] = b[:, 128 * t : 128 * t + 128]
-        for t in range(sides):
-            leave(g, t).start()
-
+    xb_ref[...] = split(jnp.concatenate(inverse[panels // 2 :], 0))
+    lax.fori_loop(0, groups, lambda g, c: (apply(g, 1, xb_ref, C), c)[1], 0, unroll=4)
     for g in range(groups):
         for t in range(sides):
-            leave(g, t).wait()
+            for part in range(2):
+                leave(g, t, part).wait()
 
 
 def finish(gram, mhl, rows, cols):
@@ -300,8 +326,9 @@
         out_specs=[far, near],
         scratch_shapes=[
             pltpu.VMEM((groups, cols // 128, C * 8, 128), F32),
-            pltpu.VMEM((2 * C, 2 * C), BF16),
-            pltpu.SemaphoreType.DMA((groups, cols // 128)),
+            pltpu.VMEM((C, C), BF16),
+            pltpu.VMEM((C, 2 * C), BF16),
+            pltpu.SemaphoreType.DMA((groups, cols // 128, 2)),
         ],
         compiler_params=pltpu.CompilerParams(vmem_limit_bytes=40 << 20),
     )(gram, mhl)

time: 70.9 us -> 65.7 us (0.927)
  Pallas kernels: 21.4 us -> 16.2 us
    pallas_call x1, Pallas kernels: 7.92 us -> 4.8 us  [columns_and_gram(): pl.pallas_call(lambda *refs: gram_kernel(rows, cols, scale, *refs), name=...]
    pallas_call x1, Pallas kernels: 10.6 us -> 8.46 us  [finish(): pl.pallas_call(lambda *refs: finish_kernel(rows, cols, *refs), name='fini...]
where the time goes in v3:
time: 65.7 us; the launch traced here: 64.6 us
  starting transfers between devices  32.1 us (49%)
  Pallas kernels  16.2 us (25%)
  waiting for transfers between devices  15.4 us (23%)
  between operations  0.86 us (1%)
    ppermute x11, starting transfers between devices, exchanged(): return lax.ppermute(value, ('gx', 'gy'), pairs)  21.6 us
    ppermute x11, waiting for transfers between devices, exchanged(): return lax.ppermute(value, ('gx', 'gy'), pairs)  11.8 us
    ppermute x4, starting transfers between devices, send(): return lax.ppermute(value, axis, up if forward else [(j, i) for i, j in up])  10.5 us
    pallas_call x1, Pallas kernels, finish(): pl.pallas_call(lambda *refs: finish_kernel(rows, cols, *refs), name='fini...  8.46 us
    pallas_call x1, Pallas kernels, columns_and_gram(): pl.pallas_call(lambda *refs: gram_kernel(rows, cols, scale, *refs), name=...  4.8 us
    ppermute x4, waiting for transfers between devices, send(): return lax.ppermute(value, axis, up if forward else [(j, i) for i, j in up])  3.59 us
    pallas_call x1, Pallas kernels, edges(): pl.pallas_call(lambda *refs: edges_kernel(rows, cols, *refs), name='edges...  2.92 us
  transfers between devices with their start and end apart: 15, of which 11 were waited for; matrix products, arithmetic and copies ran while one was open for 0% of the time, Pallas kernels for 0%

profile of v3, /device:TPU:32, one launch (start us, length us, event | category | flops | bytes accessed | tf_op | source)
XLA Modules:
  0.0 64.6 jit_solution(1814720821416259900)
XLA Ops:
  0.6 2.9 %edges.1 = (f32[40,256]{1,0:T(8,128)S(1)}, f32[40,256]{1,0:T(8,128)S(1)}, f32[40,128]{1,0:T(8,128)S(1)}, f32[40,128]{1,0:T(8,128)S(1)}, f32[2048,256]{1,0:T(8,12...) custom-call(f32[32,64,256]{2,1,0:T(8,128)} %refs_0_.1, f32[64,256]{1,0:T(8,128)} %refs_1_.1, f32[64,256]{1,0:T(8,128)} %refs_2_.1), custom_call_target="tpu_custom_call" | custom-call | tf_op jit(solution)/shard_map/edges/pallas_call | solution.py:74
  3.6 3.4 %collective-permute-start = (f32[40,256]{1,0:T(8,128)S(1)}, f32[40,256]{1,0:T(8,128)S(1)}, u32[]{:S(2)}, u32[]{:S(2)}) collective-permute-start(f32[40,256]{1,0:T(8,128)S(1)} %get-tuple-element.14), channel_id=1, source_target_pairs={{0,8},{8,16},{16,24},{24,32},{32,40},{40,48},{48,56},{56,64},{64,7... | collective-permute-start | bytes 122888 | tf_op jit(solution)/shard_map/ppermute | solution.py:364
  7.0 4.6 %collective-permute-start.1 = (f32[40,256]{1,0:T(8,128)S(1)}, f32[40,256]{1,0:T(8,128)S(1)}, u32[]{:S(2)}, u32[]{:S(2)}) collective-permute-start(f32[40,256]{1,0:T(8,128)S(1)} %get-tuple-element.15), channel_id=1, source_target_pairs={{8,0},{16,8},{24,16},{32,24},{40,32},{48,40},{56,48},{64,56},{72,6... | collective-permute-start | bytes 122888 | tf_op jit(solution)/shard_map/ppermute | solution.py:364
  11.5 1.3 %collective-permute-start.2 = (f32[40,128]{1,0:T(8,128)S(1)}, f32[40,128]{1,0:T(8,128)S(1)}, u32[]{:S(2)}, u32[]{:S(2)}) collective-permute-start(f32[40,128]{1,0:T(8,128)S(1)} %get-tuple-element.16), channel_id=1, source_target_pairs={{0,1},{1,2},{2,3},{3,4},{4,5},{5,6},{6,7},{8,9},{9,10},{10,11},{11... | collective-permute-start | bytes 61448 | tf_op jit(solution)/shard_map/ppermute | solution.py:364
  12.8 1.3 %collective-permute-start.3 = (f32[40,128]{1,0:T(8,128)S(1)}, f32[40,128]{1,0:T(8,128)S(1)}, u32[]{:S(2)}, u32[]{:S(2)}) collective-permute-start(f32[40,128]{1,0:T(8,128)S(1)} %get-tuple-element.17), channel_id=1, source_target_pairs={{1,0},{2,1},{3,2},{4,3},{5,4},{6,5},{7,6},{9,8},{10,9},{11,10},{12... | collective-permute-start | bytes 61448 | tf_op jit(solution)/shard_map/ppermute | solution.py:364
  14.1 0.0 collective-permute-done.2.refs_5_
  14.1 3.6 %collective-permute-done.3.refs_6_ = f32[40,128]{1,0:T(8,128)S(1)} collective-permute-done((f32[40,128]{1,0:T(8,128)S(1)}, f32[40,128]{1,0:T(8,128)S(1)}, u32[]{:S(2)}, u32[]{:S(2)}) %collective-permute-start.3) | collective-permute-done | bytes 20512 | tf_op jit(solution)/shard_map/ppermute | solution.py:364
  17.7 0.0 collective-permute-done.refs_3_
  17.7 0.0 collective-permute-done.1.refs_4_
  17.7 4.8 %gram.1 = (f32[80,128]{1,0:T(8,128)S(1)}, bf16[256,16384]{1,0:T(8,128)(2,1)S(1)}) custom-call(f32[2048,256]{1,0:T(8,128)S(1)} %get-tuple-element.11.refs_0_, f32[64,256]{1,0:T(8,128)S(1)} %get-tuple-element.12.refs_1_, f32[64,256]{1,0:T(8,128)S(1)} %get-tuple-element.13.refs_2_, f32[40,256]{1,0:T(8,128)S(1)} %collective-permute-done.refs_3_, ...), custom_call_target="tpu_custom_call" | custom-call | tf_op jit(solution)/shard_map/gram/pallas_call | solution.py:192
  22.5 2.6 %collective-permute-start.4 = (f32[80,128]{1,0:T(8,128)S(1)}, f32[80,128]{1,0:T(8,128)S(1)}, u32[]{:S(2)}, u32[]{:S(2)}) collective-permute-start(f32[80,128]{1,0:T(8,128)S(1)} %get-tuple-element.18), channel_id=1, source_target_pairs={{0,1},{1,0},{2,3},{3,2},{4,5},{5,4},{6,7},{7,6},{8,9},{9,8},{10,11... | collective-permute-start | bytes 122888 | tf_op jit(solution)/shard_map/ppermute | solution.py:344
  25.1 0.9 %collective-permute-done.4 = f32[80,128]{1,0:T(8,128)S(1)} collective-permute-done((f32[80,128]{1,0:T(8,128)S(1)}, f32[80,128]{1,0:T(8,128)S(1)}, u32[]{:S(2)}, u32[]{:S(2)}) %collective-permute-start.4) | collective-permute-done | bytes 40992 | tf_op jit(solution)/shard_map/ppermute | solution.py:344
  26.0 0.6 collective-permute-start.7
  26.7 0.8 %collective-permute-start.6 = (f32[80,128]{1,0:T(8,128)S(1)}, f32[80,128]{1,0:T(8,128)S(1)}, u32[]{:S(2)}, u32[]{:S(2)}) collective-permute-start(f32[80,128]{1,0:T(8,128)S(1)} %add.33), channel_id=1, source_target_pairs={{0,16},{1,5},{2,18},{3,7},{4,20},{5,1},{6,22},{7,3},{8,24},{9,13},... | collective-permute-start | bytes 122888 | tf_op jit(solution)/shard_map/ppermute | solution.py:344
  27.5 2.6 %collective-permute-start.5 = (f32[80,128]{1,0:T(8,128)S(1)}, f32[80,128]{1,0:T(8,128)S(1)}, u32[]{:S(2)}, u32[]{:S(2)}) collective-permute-start(f32[80,128]{1,0:T(8,128)S(1)} %add.33), channel_id=1, source_target_pairs={{0,8},{1,3},{2,10},{3,1},{4,12},{5,7},{6,14},{7,5},{8,0},{9,11},{1... | collective-permute-start | bytes 122888 | tf_op jit(solution)/shard_map/ppermute | solution.py:344
  30.1 1.1 %collective-permute-done.7 = f32[80,128]{1,0:T(8,128)S(1)} collective-permute-done((f32[80,128]{1,0:T(8,128)S(1)}, f32[80,128]{1,0:T(8,128)S(1)}, u32[]{:S(2)}, u32[]{:S(2)}) %collective-permute-start.7) | collective-permute-done | bytes 40992 | tf_op jit(solution)/shard_map/ppermute | solution.py:344
  31.2 0.9 %collective-permute-done.6 = f32[80,128]{1,0:T(8,128)S(1)} collective-permute-done((f32[80,128]{1,0:T(8,128)S(1)}, f32[80,128]{1,0:T(8,128)S(1)}, u32[]{:S(2)}, u32[]{:S(2)}) %collective-permute-start.6) | collective-permute-done | bytes 40992 | tf_op jit(solution)/shard_map/ppermute | solution.py:344
  32.2 0.4 collective-permute-done.5
  32.5 1.8 %collective-permute-start.10 = (f32[80,128]{1,0:T(8,128)S(1)}, f32[80,128]{1,0:T(8,128)S(1)}, u32[]{:S(2)}, u32[]{:S(2)}) collective-permute-start(f32[80,128]{1,0:T(8,128)S(1)} %add_add_fusion.2), channel_id=1, source_target_pairs={{0,6},{1,25},{2,4},{3,27},{4,2},{5,29},{6,0},{7,31},{8,14},{9,17},... | collective-permute-start | bytes 122888 | tf_op jit(solution)/shard_map/ppermute | solution.py:344
  34.3 2.0 %collective-permute-start.9 = (f32[80,128]{1,0:T(8,128)S(1)}, f32[80,128]{1,0:T(8,128)S(1)}, u32[]{:S(2)}, u32[]{:S(2)}) collective-permute-start(f32[80,128]{1,0:T(8,128)S(1)} %add_add_fusion.2), channel_id=1, source_target_pairs={{0,4},{1,17},{2,6},{3,19},{4,0},{5,21},{6,2},{7,23},{8,12},{9,25},... | collective-permute-start | bytes 122888 | tf_op jit(solution)/shard_map/ppermute | solution.py:344
  36.3 0.4 collective-permute-start.8
  36.7 1.1 %collective-permute-done.10 = f32[80,128]{1,0:T(8,128)S(1)} collective-permute-done((f32[80,128]{1,0:T(8,128)S(1)}, f32[80,128]{1,0:T(8,128)S(1)}, u32[]{:S(2)}, u32[]{:S(2)}) %collective-permute-start.10) | collective-permute-done | bytes 40992 | tf_op jit(solution)/shard_map/ppermute | solution.py:344
  37.8 2.0 %collective-permute-done.9 = f32[80,128]{1,0:T(8,128)S(1)} collective-permute-done((f32[80,128]{1,0:T(8,128)S(1)}, f32[80,128]{1,0:T(8,128)S(1)}, u32[]{:S(2)}, u32[]{:S(2)}) %collective-permute-start.9) | collective-permute-done | bytes 40992 | tf_op jit(solution)/shard_map/ppermute | solution.py:344
  39.8 0.4 collective-permute-done.8
  40.3 2.0 %collective-permute-start.13 = (f32[80,128]{1,0:T(8,128)S(1)}, f32[80,128]{1,0:T(8,128)S(1)}, u32[]{:S(2)}, u32[]{:S(2)}) collective-permute-start(f32[80,128]{1,0:T(8,128)S(1)} %add_add_fusion.1), channel_id=1, source_target_pairs={{0,96},{1,97},{2,98},{3,99},{4,100},{5,101},{6,102},{7,103},{8,104... | collective-permute-start | bytes 122888 | tf_op jit(solution)/shard_map/ppermute | solution.py:344
  42.3 2.1 %collective-permute-start.12 = (f32[80,128]{1,0:T(8,128)S(1)}, f32[80,128]{1,0:T(8,128)S(1)}, u32[]{:S(2)}, u32[]{:S(2)}) collective-permute-start(f32[80,128]{1,0:T(8,128)S(1)} %add_add_fusion.1), channel_id=1, source_target_pairs={{0,64},{1,65},{2,66},{3,67},{4,68},{5,69},{6,70},{7,71},{8,72},{9,... | collective-permute-start | bytes 122888 | tf_op jit(solution)/shard_map/ppermute | solution.py:344
  44.4 1.4 %collective-permute-start.11 = (f32[80,128]{1,0:T(8,128)S(1)}, f32[80,128]{1,0:T(8,128)S(1)}, u32[]{:S(2)}, u32[]{:S(2)}) collective-permute-start(f32[80,128]{1,0:T(8,128)S(1)} %add_add_fusion.1), channel_id=1, source_target_pairs={{0,32},{1,33},{2,34},{3,35},{4,36},{5,37},{6,38},{7,39},{8,40},{9,... | collective-permute-start | bytes 122888 | tf_op jit(solution)/shard_map/ppermute | solution.py:344
  45.8 0.0 collective-permute-done.13
  45.8 1.4 %collective-permute-done.12 = f32[80,128]{1,0:T(8,128)S(1)} collective-permute-done((f32[80,128]{1,0:T(8,128)S(1)}, f32[80,128]{1,0:T(8,128)S(1)}, u32[]{:S(2)}, u32[]{:S(2)}) %collective-permute-start.12) | collective-permute-done | bytes 40992 | tf_op jit(solution)/shard_map/ppermute | solution.py:344
  47.2 1.4 %collective-permute-done.11 = f32[80,128]{1,0:T(8,128)S(1)} collective-permute-done((f32[80,128]{1,0:T(8,128)S(1)}, f32[80,128]{1,0:T(8,128)S(1)}, u32[]{:S(2)}, u32[]{:S(2)}) %collective-permute-start.11) | collective-permute-done | bytes 40992 | tf_op jit(solution)/shard_map/ppermute | solution.py:344
  48.6 5.2 %collective-permute-start.14 = (f32[80,128]{1,0:T(8,128)S(1)}, f32[80,128]{1,0:T(8,128)S(1)}, u32[]{:S(2)}, u32[]{:S(2)}) collective-permute-start(f32[80,128]{1,0:T(8,128)S(1)} %add_add_fusion), channel_id=1, source_target_pairs={{0,224},{1,225},{2,226},{3,227},{4,228},{5,229},{6,230},{7,231},{8... | collective-permute-start | bytes 122888 | tf_op jit(solution)/shard_map/ppermute | solution.py:344
  53.9 2.1 %collective-permute-done.14 = f32[80,128]{1,0:T(8,128)S(1)} collective-permute-done((f32[80,128]{1,0:T(8,128)S(1)}, f32[80,128]{1,0:T(8,128)S(1)}, u32[]{:S(2)}, u32[]{:S(2)}) %collective-permute-start.14) | collective-permute-done | bytes 40992 | tf_op jit(solution)/shard_map/ppermute | solution.py:344
  56.0 8.5 %finish.1 = (f32[128,64,256]{2,1,0:T(8,128)}, f32[128,128]{1,0:T(8,128)}) custom-call(f32[80,128]{1,0:T(8,128)S(1)} %add.43.refs_0_, bf16[256,16384]{1,0:T(8,128)(2,1)S(1)} %get-tuple-element.19.refs_1_), custom_call_target="tpu_custom_call" | custom-call | tf_op jit(solution)/shard_map/finish/pallas_call | solution.py:321
  (5 shorter events, 0.1 us)
Async XLA Ops:
  3.6 14.2 %collective-permute-start = (f32[40,256]{1,0:T(8,128)S(1)}, f32[40,256]{1,0:T(8,128)S(1)}, u32[]{:S(2)}, u32[]{:S(2)}) collective-permute-start(f32[40,256]{1,0:T(8,128)S(1)} %get-tuple-element.14), channel_id=1, source_target_pairs={{0,8},{8,16},{16,24},{24,32},{32,40},{40,48},{48,56},{56,64},{64,7... | collective-permute-start | bytes 122888 | tf_op jit(solution)/shard_map/ppermute | solution.py:364
  7.0 10.8 %collective-permute-start.1 = (f32[40,256]{1,0:T(8,128)S(1)}, f32[40,256]{1,0:T(8,128)S(1)}, u32[]{:S(2)}, u32[]{:S(2)}) collective-permute-start(f32[40,256]{1,0:T(8,128)S(1)} %get-tuple-element.15), channel_id=1, source_target_pairs={{8,0},{16,8},{24,16},{32,24},{40,32},{48,40},{56,48},{64,56},{72,6... | collective-permute-start | bytes 122888 | tf_op jit(solution)/shard_map/ppermute | solution.py:364
  11.5 2.6 %collective-permute-start.2 = (f32[40,128]{1,0:T(8,128)S(1)}, f32[40,128]{1,0:T(8,128)S(1)}, u32[]{:S(2)}, u32[]{:S(2)}) collective-permute-start(f32[40,128]{1,0:T(8,128)S(1)} %get-tuple-element.16), channel_id=1, source_target_pairs={{0,1},{1,2},{2,3},{3,4},{4,5},{5,6},{6,7},{8,9},{9,10},{10,11},{11... | collective-permute-start | bytes 61448 | tf_op jit(solution)/shard_map/ppermute | solution.py:364
  12.8 4.9 %collective-permute-start.3 = (f32[40,128]{1,0:T(8,128)S(1)}, f32[40,128]{1,0:T(8,128)S(1)}, u32[]{:S(2)}, u32[]{:S(2)}) collective-permute-start(f32[40,128]{1,0:T(8,128)S(1)} %get-tuple-element.17), channel_id=1, source_target_pairs={{1,0},{2,1},{3,2},{4,3},{5,4},{6,5},{7,6},{9,8},{10,9},{11,10},{12... | collective-permute-start | bytes 61448 | tf_op jit(solution)/shard_map/ppermute | solution.py:364
  22.5 3.5 %collective-permute-start.4 = (f32[80,128]{1,0:T(8,128)S(1)}, f32[80,128]{1,0:T(8,128)S(1)}, u32[]{:S(2)}, u32[]{:S(2)}) collective-permute-start(f32[80,128]{1,0:T(8,128)S(1)} %get-tuple-element.18), channel_id=1, source_target_pairs={{0,1},{1,0},{2,3},{3,2},{4,5},{5,4},{6,7},{7,6},{8,9},{9,8},{10,11... | collective-permute-start | bytes 122888 | tf_op jit(solution)/shard_map/ppermute | solution.py:344
  26.0 5.2 %collective-permute-start.7 = (f32[80,128]{1,0:T(8,128)S(1)}, f32[80,128]{1,0:T(8,128)S(1)}, u32[]{:S(2)}, u32[]{:S(2)}) collective-permute-start(f32[80,128]{1,0:T(8,128)S(1)} %add.33), channel_id=1, source_target_pairs={{0,24},{1,7},{2,26},{3,5},{4,28},{5,3},{6,30},{7,1},{8,16},{9,15},... | collective-permute-start | bytes 122888 | tf_op jit(solution)/shard_map/ppermute | solution.py:344
  26.7 5.5 %collective-permute-start.6 = (f32[80,128]{1,0:T(8,128)S(1)}, f32[80,128]{1,0:T(8,128)S(1)}, u32[]{:S(2)}, u32[]{:S(2)}) collective-permute-start(f32[80,128]{1,0:T(8,128)S(1)} %add.33), channel_id=1, source_target_pairs={{0,16},{1,5},{2,18},{3,7},{4,20},{5,1},{6,22},{7,3},{8,24},{9,13},... | collective-permute-start | bytes 122888 | tf_op jit(solution)/shard_map/ppermute | solution.py:344
  27.5 5.1 %collective-permute-start.5 = (f32[80,128]{1,0:T(8,128)S(1)}, f32[80,128]{1,0:T(8,128)S(1)}, u32[]{:S(2)}, u32[]{:S(2)}) collective-permute-start(f32[80,128]{1,0:T(8,128)S(1)} %add.33), channel_id=1, source_target_pairs={{0,8},{1,3},{2,10},{3,1},{4,12},{5,7},{6,14},{7,5},{8,0},{9,11},{1... | collective-permute-start | bytes 122888 | tf_op jit(solution)/shard_map/ppermute | solution.py:344
  32.5 5.3 %collective-permute-start.10 = (f32[80,128]{1,0:T(8,128)S(1)}, f32[80,128]{1,0:T(8,128)S(1)}, u32[]{:S(2)}, u32[]{:S(2)}) collective-permute-start(f32[80,128]{1,0:T(8,128)S(1)} %add_add_fusion.2), channel_id=1, source_target_pairs={{0,6},{1,25},{2,4},{3,27},{4,2},{5,29},{6,0},{7,31},{8,14},{9,17},... | collective-permute-start | bytes 122888 | tf_op jit(solution)/shard_map/ppermute | solution.py:344
  34.3 5.5 %collective-permute-start.9 = (f32[80,128]{1,0:T(8,128)S(1)}, f32[80,128]{1,0:T(8,128)S(1)}, u32[]{:S(2)}, u32[]{:S(2)}) collective-permute-start(f32[80,128]{1,0:T(8,128)S(1)} %add_add_fusion.2), channel_id=1, source_target_pairs={{0,4},{1,17},{2,6},{3,19},{4,0},{5,21},{6,2},{7,23},{8,12},{9,25},... | collective-permute-start | bytes 122888 | tf_op jit(solution)/shard_map/ppermute | solution.py:344
  36.3 4.0 %collective-permute-start.8 = (f32[80,128]{1,0:T(8,128)S(1)}, f32[80,128]{1,0:T(8,128)S(1)}, u32[]{:S(2)}, u32[]{:S(2)}) collective-permute-start(f32[80,128]{1,0:T(8,128)S(1)} %add_add_fusion.2), channel_id=1, source_target_pairs={{0,2},{1,9},{2,0},{3,11},{4,6},{5,13},{6,4},{7,15},{8,10},{9,1},{1... | collective-permute-start | bytes 122888 | tf_op jit(solution)/shard_map/ppermute | solution.py:344
  40.3 5.5 %collective-permute-start.13 = (f32[80,128]{1,0:T(8,128)S(1)}, f32[80,128]{1,0:T(8,128)S(1)}, u32[]{:S(2)}, u32[]{:S(2)}) collective-permute-start(f32[80,128]{1,0:T(8,128)S(1)} %add_add_fusion.1), channel_id=1, source_target_pairs={{0,96},{1,97},{2,98},{3,99},{4,100},{5,101},{6,102},{7,103},{8,104... | collective-permute-start | bytes 122888 | tf_op jit(solution)/shard_map/ppermute | solution.py:344
  42.3 4.9 %collective-permute-start.12 = (f32[80,128]{1,0:T(8,128)S(1)}, f32[80,128]{1,0:T(8,128)S(1)}, u32[]{:S(2)}, u32[]{:S(2)}) collective-permute-start(f32[80,128]{1,0:T(8,128)S(1)} %add_add_fusion.1), channel_id=1, source_target_pairs={{0,64},{1,65},{2,66},{3,67},{4,68},{5,69},{6,70},{7,71},{8,72},{9,... | collective-permute-start | bytes 122888 | tf_op jit(solution)/shard_map/ppermute | solution.py:344
  44.4 4.2 %collective-permute-start.11 = (f32[80,128]{1,0:T(8,128)S(1)}, f32[80,128]{1,0:T(8,128)S(1)}, u32[]{:S(2)}, u32[]{:S(2)}) collective-permute-start(f32[80,128]{1,0:T(8,128)S(1)} %add_add_fusion.1), channel_id=1, source_target_pairs={{0,32},{1,33},{2,34},{3,35},{4,36},{5,37},{6,38},{7,39},{8,40},{9,... | collective-permute-start | bytes 122888 | tf_op jit(solution)/shard_map/ppermute | solution.py:344
  48.6 7.3 %collective-permute-start.14 = (f32[80,128]{1,0:T(8,128)S(1)}, f32[80,128]{1,0:T(8,128)S(1)}, u32[]{:S(2)}, u32[]{:S(2)}) collective-permute-start(f32[80,128]{1,0:T(8,128)S(1)} %add_add_fusion), channel_id=1, source_target_pairs={{0,224},{1,225},{2,226},{3,227},{4,228},{5,229},{6,230},{7,231},{8... | collective-permute-start | bytes 122888 | tf_op jit(solution)/shard_map/ppermute | solution.py:344

commit v4 on v3

--- a/solution.py
+++ b/solution.py
@@ -17,7 +17,7 @@
 
 
 def edges_kernel(
-    rows, cols, u_ref, k_ref, v_ref, top_ref, bottom_ref, left_ref, right_ref, rows_ref, ko_ref, vo_ref, buf, u_sem, c_sem
+    rows, cols, u_ref, k_ref, v_ref, x1_ref, x2_ref, y1_ref, y2_ref, rows_ref, ko_ref, vo_ref, buf, u_sem, c_sem
 ):
     sides = cols // 128
     groups = rows // 8
@@ -27,6 +27,8 @@
             u_ref.at[:, pl.ds(pl.multiple_of(8 * g, 8), 8), 128 * t : 128 * t + 128], buf.at[g, t].reshape(K, 8, 128), u_sem.at[g, t]
         )
 
+    even_x = lax.axis_index("gx") % 2 == 0
+    even_y = lax.axis_index("gy") % 2 == 0
     k_copy = pltpu.make_async_copy(k_ref, ko_ref, c_sem.at[0])
     v_copy = pltpu.make_async_copy(v_ref, vo_ref, c_sem.at[1])
     k_copy.start()
@@ -48,11 +50,10 @@
         for t in range(sides):
             rows_ref[K * i : K * i + K, 128 * t : 128 * t + 128] = parts[t]
         conduct = jnp.broadcast_to(ko_ref[i : i + 1, :], (8, cols))
-        for ref, at in ((top_ref, 0), (bottom_ref, rows - 1)):
-            if i == at:
-                for t in range(sides):
-                    ref[:K, 128 * t : 128 * t + 128] = parts[t]
-                ref[K:, :] = conduct
+        if i == 0:
+            top = jnp.concatenate([jnp.concatenate(parts, 1), conduct], 0)
+        if i == rows - 1:
+            bottom = jnp.concatenate([jnp.concatenate(parts, 1), conduct], 0)
         for b in range(K // 8 + 1):
             if b == K // 8:
                 first, last = conduct[:, :128], conduct[:, cols - 128 :]
@@ -61,8 +62,10 @@
             left[b] = jnp.where(here, pltpu.roll(first, i, 1) if i else first, left[b])
             right[b] = jnp.where(here, pltpu.roll(last, (i + 1) % 128, 1), right[b])
     for b in range(K // 8 + 1):
-        left_ref[8 * b : 8 * b + 8, :] = left[b]
-        right_ref[8 * b : 8 * b + 8, :] = right[b]
+        y1_ref[8 * b : 8 * b + 8, :] = jnp.where(even_y, right[b], left[b])
+        y2_ref[8 * b : 8 * b + 8, :] = jnp.where(even_y, left[b], right[b])
+    x1_ref[...] = jnp.where(even_x, bottom, top)
+    x2_ref[...] = jnp.where(even_x, top, bottom)
     v_copy.wait()
 
 
@@ -86,7 +89,9 @@
     )(*[pltpu.with_memory_space_constraint(a, pltpu.HBM) for a in (fields, conduct, potential)])
 
 
-def gram_kernel(rows, cols, scale, u_ref, k_ref, v_ref, up_ref, dn_ref, lf_ref, rt_ref, gram_ref, mhl_ref, acc_ref):
+def gram_kernel(
+    rows, cols, places, scale, u_ref, k_ref, v_ref, x1_ref, x2_ref, y1_ref, y2_ref, gram_ref, mhl_ref, acc_ref, lf_ref, rt_ref
+):
     per = 8
     wide = per * cols
     lane = iota((K, 128), 1)
@@ -110,6 +115,14 @@
     def spread(row):
         return jnp.broadcast_to(row[0:1, :], (K, 128))
 
+    def from_neighbours(axis, first, second):
+        at, last = lax.axis_index(axis), places[axis] - 1
+        even = at % 2 == 0
+        before = jnp.where(at == 0, 0.0, jnp.where(even, second, first))
+        return before, jnp.where(at == last, 0.0, jnp.where(even, first, second))
+
+    up, down = from_neighbours("gx", x1_ref[...], x2_ref[...])
+    lf_ref[...], rt_ref[...] = from_neighbours("gy", y1_ref[...], y2_ref[...])
     acc_ref[...] = jnp.zeros_like(acc_ref)
 
     @pl.loop(0, rows // per, unroll=True)
@@ -119,10 +132,10 @@
         is_last = step == rows // per - 1
         i_before = jnp.maximum(base - 1, 0)
         i_after = jnp.minimum(base + per, rows - 1)
-        u_before = jnp.where(is_first, up_ref[:K], field(i_before))
-        k_before = jnp.where(is_first, up_ref[K : K + 1], k_ref[pl.ds(i_before, 1), :])
-        u_after = jnp.where(is_last, dn_ref[:K], field(i_after))
-        k_after = jnp.where(is_last, dn_ref[K : K + 1], k_ref[pl.ds(i_after, 1), :])
+        u_before = jnp.where(is_first, up[:K], field(i_before))
+        k_before = jnp.where(is_first, up[K : K + 1], k_ref[pl.ds(i_before, 1), :])
+        u_after = jnp.where(is_last, down[:K], field(i_after))
+        k_after = jnp.where(is_last, down[K : K + 1], k_ref[pl.ds(i_after, 1), :])
         u_now = field(base)
         k_now = k_ref[pl.ds(base, 1), :]
         flux_before = [
@@ -185,17 +198,17 @@
     return jnp.where(iota((C, C), 1) // 32 >= iota((C, C), 0) // 32, upper, upper.T)
 
 
-def columns_and_gram(u_rows, conduct, potential, up, down, left, right, scale):
+def columns_and_gram(u_rows, conduct, potential, swapped, places, scale):
     rows, cols = conduct.shape
     near = pl.BlockSpec(memory_space=pltpu.VMEM)
-    args = (u_rows, conduct, potential, up, down, left, right)
+    args = (u_rows, conduct, potential, *swapped)
     return pl.pallas_call(
-        lambda *refs: gram_kernel(rows, cols, scale, *refs),
+        lambda *refs: gram_kernel(rows, cols, places, scale, *refs),
         name="gram",
         out_shape=[jax.ShapeDtypeStruct((80, C), F32), jax.ShapeDtypeStruct((2 * C, rows * cols), BF16)],
         in_specs=[near] * len(args),
         out_specs=[near] * 2,
-        scratch_shapes=[pltpu.VMEM((C, 2 * C), F32)],
+        scratch_shapes=[pltpu.VMEM((C, 2 * C), F32)] + [pltpu.VMEM((K + 8, 128), F32)] * 2,
         compiler_params=pltpu.CompilerParams(vmem_limit_bytes=32 << 20),
     )(*args)
 
@@ -356,19 +369,21 @@
 
 def on_device(mode_fields, conductance, potential):
     fields, rows, cols = mode_fields.shape
-    top, bottom, left, right, u_rows, conduct, potent = edges(mode_fields, conductance, potential)
-
-    def send(value, axis, forward):
-        peers = lax.axis_size(axis)
-        up = [(i, i + 1) for i in range(peers - 1)]
-        return lax.ppermute(value, axis, up if forward else [(j, i) for i, j in up])
-
-    from_up = send(bottom, "gx", True)
-    from_down = send(top, "gx", False)
-    from_left = send(right, "gy", True)
-    from_right = send(left, "gy", False)
-    cells = rows * cols * lax.axis_size("gx") * lax.axis_size("gy")
-    gram, mhl = columns_and_gram(u_rows, conduct, potent, from_up, from_down, from_left, from_right, 1.0 / cells)
+    along_x1, along_x2, along_y1, along_y2, u_rows, conduct, potent = edges(mode_fields, conductance, potential)
+    places = {axis: lax.axis_size(axis) for axis in ("gx", "gy")}
+
+    def swap(value, axis, first):
+        n = places[axis]
+        return lax.ppermute(value, axis, [(i, (i + 1 if (i % 2 == 0) == first else i - 1) % n) for i in range(n)])
+
+    swapped = (
+        swap(along_x1, "gx", True),
+        swap(along_x2, "gx", False),
+        swap(along_y1, "gy", True),
+        swap(along_y2, "gy", False),
+    )
+    cells = rows * cols * places["gx"] * places["gy"]
+    gram, mhl = columns_and_gram(u_rows, conduct, potent, swapped, places, 1.0 / cells)
     basis_field, scaled_factor = finish(sum_over_devices(gram), mhl, rows, cols)
     return (basis_field, scaled_factor)
 

time: 65.7 us -> 60.8 us (0.925); the launches traced: 64.6 us -> 60.6 us
  starting transfers between devices: 32.1 us -> 24.3 us
  waiting for transfers between devices: 15.4 us -> 19.3 us
    ppermute x11, waiting for transfers between devices: 11.8 us -> 17.8 us  [exchanged(): return lax.ppermute(value, ('gx', 'gy'), pairs)]
    ppermute x4, starting transfers between devices: 10.5 us -> 6.35 us  [swap(): lax.ppermute(value, axis, [(i, (i + 1 if (i % 2 == 0) == first else i - 1...]
    ppermute x11, starting transfers between devices: 21.6 us -> 18 us  [exchanged(): return lax.ppermute(value, ('gx', 'gy'), pairs)]
    ppermute x4, waiting for transfers between devices: 3.59 us -> 1.49 us  [swap(): lax.ppermute(value, axis, [(i, (i + 1 if (i % 2 == 0) == first else i - 1...]
  transfers between devices with their start and end apart: 15 -> 15, of which waited for: 11 -> 9; matrix products, arithmetic and copies ran while one was open for 0% -> 0% of each run, Pallas kernels for 0% -> 0%
where the time goes in v4:
time: 60.8 us; the launch traced here: 60.6 us
  starting transfers between devices  24.3 us (40%)
  waiting for transfers between devices  19.3 us (32%)
  Pallas kernels  16.1 us (26%)
  between operations  0.83 us (1%)
    ppermute x11, starting transfers between devices, exchanged(): return lax.ppermute(value, ('gx', 'gy'), pairs)  18 us
    ppermute x11, waiting for transfers between devices, exchanged(): return lax.ppermute(value, ('gx', 'gy'), pairs)  17.8 us
    pallas_call x1, Pallas kernels, finish(): pl.pallas_call(lambda *refs: finish_kernel(rows, cols, *refs), name='fini...  8.46 us
    ppermute x4, starting transfers between devices, swap(): lax.ppermute(value, axis, [(i, (i + 1 if (i % 2 == 0) == first else i - 1...  6.35 us
    pallas_call x1, Pallas kernels, columns_and_gram(): pl.pallas_call(lambda *refs: gram_kernel(rows, cols, places, scale, *refs...  4.74 us
    pallas_call x1, Pallas kernels, edges(): pl.pallas_call(lambda *refs: edges_kernel(rows, cols, *refs), name='edges...  2.92 us
    ppermute x4, waiting for transfers between devices, swap(): lax.ppermute(value, axis, [(i, (i + 1 if (i % 2 == 0) == first else i - 1...  1.49 us
  transfers between devices with their start and end apart: 15, of which 9 were waited for; matrix products, arithmetic and copies ran while one was open for 0% of the time, Pallas kernels for 0%

profile of v4, /device:TPU:32, one launch (start us, length us, event | category | flops | bytes accessed | tf_op | source)
XLA Modules:
  0.0 60.6 jit_solution(4692227322244108735)
XLA Ops:
  0.6 2.9 %edges.1 = (f32[40,256]{1,0:T(8,128)S(1)}, f32[40,256]{1,0:T(8,128)S(1)}, f32[40,128]{1,0:T(8,128)S(1)}, f32[40,128]{1,0:T(8,128)S(1)}, f32[2048,256]{1,0:T(8,12...) custom-call(f32[32,64,256]{2,1,0:T(8,128)} %refs_0_.1, f32[64,256]{1,0:T(8,128)} %refs_1_.1, f32[64,256]{1,0:T(8,128)} %refs_2_.1), custom_call_target="tpu_custom_call" | custom-call | tf_op jit(solution)/shard_map/edges/pallas_call | solution.py:77
  3.6 1.6 %collective-permute-start = (f32[40,256]{1,0:T(8,128)S(1)}, f32[40,256]{1,0:T(8,128)S(1)}, u32[]{:S(2)}, u32[]{:S(2)}) collective-permute-start(f32[40,256]{1,0:T(8,128)S(1)} %get-tuple-element.14), channel_id=1, source_target_pairs={{0,8},{8,0},{16,24},{24,16},{32,40},{40,32},{48,56},{56,48},{64,72... | collective-permute-start | bytes 122888 | tf_op jit(solution)/shard_map/ppermute | solution.py:377
  5.1 1.6 %collective-permute-start.1 = (f32[40,256]{1,0:T(8,128)S(1)}, f32[40,256]{1,0:T(8,128)S(1)}, u32[]{:S(2)}, u32[]{:S(2)}) collective-permute-start(f32[40,256]{1,0:T(8,128)S(1)} %get-tuple-element.15), channel_id=1, source_target_pairs={{0,248},{8,16},{16,8},{24,32},{32,24},{40,48},{48,40},{56,64},{64,... | collective-permute-start | bytes 122888 | tf_op jit(solution)/shard_map/ppermute | solution.py:377
  6.8 0.0 collective-permute-start.2
  6.8 3.1 %collective-permute-start.3 = (f32[40,128]{1,0:T(8,128)S(1)}, f32[40,128]{1,0:T(8,128)S(1)}, u32[]{:S(2)}, u32[]{:S(2)}) collective-permute-start(f32[40,128]{1,0:T(8,128)S(1)} %get-tuple-element.17), channel_id=1, source_target_pairs={{0,7},{1,2},{2,1},{3,4},{4,3},{5,6},{6,5},{7,0},{8,15},{9,10},{10,... | collective-permute-start | bytes 61448 | tf_op jit(solution)/shard_map/ppermute | solution.py:377
  9.9 0.0 collective-permute-done.2.refs_5_
  9.9 1.5 %collective-permute-done.3.refs_6_ = f32[40,128]{1,0:T(8,128)S(1)} collective-permute-done((f32[40,128]{1,0:T(8,128)S(1)}, f32[40,128]{1,0:T(8,128)S(1)}, u32[]{:S(2)}, u32[]{:S(2)}) %collective-permute-start.3) | collective-permute-done | bytes 20512 | tf_op jit(solution)/shard_map/ppermute | solution.py:377
  11.4 0.0 collective-permute-done.refs_3_
  11.4 0.0 collective-permute-done.1.refs_4_
  11.4 4.7 %gram.1 = (f32[80,128]{1,0:T(8,128)S(1)}, bf16[256,16384]{1,0:T(8,128)(2,1)S(1)}) custom-call(f32[2048,256]{1,0:T(8,128)S(1)} %get-tuple-element.11.refs_0_, f32[64,256]{1,0:T(8,128)S(1)} %get-tuple-element.12.refs_1_, f32[64,256]{1,0:T(8,128)S(1)} %get-tuple-element.13.refs_2_, f32[40,256]{1,0:T(8,128)S(1)} %collective-permute-done.refs_3_, ...), custom_call_target="tpu_custom_call" | custom-call | tf_op jit(solution)/shard_map/gram/pallas_call | solution.py:205
  16.1 0.1 collective-permute-start.4
  16.2 1.2 %collective-permute-done.4 = f32[80,128]{1,0:T(8,128)S(1)} collective-permute-done((f32[80,128]{1,0:T(8,128)S(1)}, f32[80,128]{1,0:T(8,128)S(1)}, u32[]{:S(2)}, u32[]{:S(2)}) %collective-permute-start.4) | collective-permute-done | bytes 40992 | tf_op jit(solution)/shard_map/ppermute | solution.py:357
  17.5 2.9 %collective-permute-start.7 = (f32[80,128]{1,0:T(8,128)S(1)}, f32[80,128]{1,0:T(8,128)S(1)}, u32[]{:S(2)}, u32[]{:S(2)}) collective-permute-start(f32[80,128]{1,0:T(8,128)S(1)} %add.33), channel_id=1, source_target_pairs={{0,24},{1,7},{2,26},{3,5},{4,28},{5,3},{6,30},{7,1},{8,16},{9,15},... | collective-permute-start | bytes 122888 | tf_op jit(solution)/shard_map/ppermute | solution.py:357
  20.4 0.2 collective-permute-start.6
  20.6 1.0 %collective-permute-start.5 = (f32[80,128]{1,0:T(8,128)S(1)}, f32[80,128]{1,0:T(8,128)S(1)}, u32[]{:S(2)}, u32[]{:S(2)}) collective-permute-start(f32[80,128]{1,0:T(8,128)S(1)} %add.33), channel_id=1, source_target_pairs={{0,8},{1,3},{2,10},{3,1},{4,12},{5,7},{6,14},{7,5},{8,0},{9,11},{1... | collective-permute-start | bytes 122888 | tf_op jit(solution)/shard_map/ppermute | solution.py:357
  21.6 1.1 %collective-permute-done.7 = f32[80,128]{1,0:T(8,128)S(1)} collective-permute-done((f32[80,128]{1,0:T(8,128)S(1)}, f32[80,128]{1,0:T(8,128)S(1)}, u32[]{:S(2)}, u32[]{:S(2)}) %collective-permute-start.7) | collective-permute-done | bytes 40992 | tf_op jit(solution)/shard_map/ppermute | solution.py:357
  22.7 3.2 %collective-permute-done.6 = f32[80,128]{1,0:T(8,128)S(1)} collective-permute-done((f32[80,128]{1,0:T(8,128)S(1)}, f32[80,128]{1,0:T(8,128)S(1)}, u32[]{:S(2)}, u32[]{:S(2)}) %collective-permute-start.6) | collective-permute-done | bytes 40992 | tf_op jit(solution)/shard_map/ppermute | solution.py:357
  25.9 0.0 collective-permute-done.5
  25.9 3.1 %collective-permute-start.10 = (f32[80,128]{1,0:T(8,128)S(1)}, f32[80,128]{1,0:T(8,128)S(1)}, u32[]{:S(2)}, u32[]{:S(2)}) collective-permute-start(f32[80,128]{1,0:T(8,128)S(1)} %add_add_fusion.2), channel_id=1, source_target_pairs={{0,6},{1,25},{2,4},{3,27},{4,2},{5,29},{6,0},{7,31},{8,14},{9,17},... | collective-permute-start | bytes 122888 | tf_op jit(solution)/shard_map/ppermute | solution.py:357
  29.0 0.0 collective-permute-start.9
  29.0 1.1 %collective-permute-start.8 = (f32[80,128]{1,0:T(8,128)S(1)}, f32[80,128]{1,0:T(8,128)S(1)}, u32[]{:S(2)}, u32[]{:S(2)}) collective-permute-start(f32[80,128]{1,0:T(8,128)S(1)} %add_add_fusion.2), channel_id=1, source_target_pairs={{0,2},{1,9},{2,0},{3,11},{4,6},{5,13},{6,4},{7,15},{8,10},{9,1},{1... | collective-permute-start | bytes 122888 | tf_op jit(solution)/shard_map/ppermute | solution.py:357
  30.1 1.1 %collective-permute-done.10 = f32[80,128]{1,0:T(8,128)S(1)} collective-permute-done((f32[80,128]{1,0:T(8,128)S(1)}, f32[80,128]{1,0:T(8,128)S(1)}, u32[]{:S(2)}, u32[]{:S(2)}) %collective-permute-start.10) | collective-permute-done | bytes 40992 | tf_op jit(solution)/shard_map/ppermute | solution.py:357
  31.2 3.3 %collective-permute-done.9 = f32[80,128]{1,0:T(8,128)S(1)} collective-permute-done((f32[80,128]{1,0:T(8,128)S(1)}, f32[80,128]{1,0:T(8,128)S(1)}, u32[]{:S(2)}, u32[]{:S(2)}) %collective-permute-start.9) | collective-permute-done | bytes 40992 | tf_op jit(solution)/shard_map/ppermute | solution.py:357
  34.5 0.0 collective-permute-done.8
  34.5 2.0 %collective-permute-start.13 = (f32[80,128]{1,0:T(8,128)S(1)}, f32[80,128]{1,0:T(8,128)S(1)}, u32[]{:S(2)}, u32[]{:S(2)}) collective-permute-start(f32[80,128]{1,0:T(8,128)S(1)} %add_add_fusion.1), channel_id=1, source_target_pairs={{0,96},{1,97},{2,98},{3,99},{4,100},{5,101},{6,102},{7,103},{8,104... | collective-permute-start | bytes 122888 | tf_op jit(solution)/shard_map/ppermute | solution.py:357
  36.5 4.4 %collective-permute-start.12 = (f32[80,128]{1,0:T(8,128)S(1)}, f32[80,128]{1,0:T(8,128)S(1)}, u32[]{:S(2)}, u32[]{:S(2)}) collective-permute-start(f32[80,128]{1,0:T(8,128)S(1)} %add_add_fusion.1), channel_id=1, source_target_pairs={{0,64},{1,65},{2,66},{3,67},{4,68},{5,69},{6,70},{7,71},{8,72},{9,... | collective-permute-start | bytes 122888 | tf_op jit(solution)/shard_map/ppermute | solution.py:357
  40.9 0.0 collective-permute-start.11
  40.9 0.0 collective-permute-done.13
  40.9 2.4 %collective-permute-done.12 = f32[80,128]{1,0:T(8,128)S(1)} collective-permute-done((f32[80,128]{1,0:T(8,128)S(1)}, f32[80,128]{1,0:T(8,128)S(1)}, u32[]{:S(2)}, u32[]{:S(2)}) %collective-permute-start.12) | collective-permute-done | bytes 40992 | tf_op jit(solution)/shard_map/ppermute | solution.py:357
  43.3 1.6 %collective-permute-done.11 = f32[80,128]{1,0:T(8,128)S(1)} collective-permute-done((f32[80,128]{1,0:T(8,128)S(1)}, f32[80,128]{1,0:T(8,128)S(1)}, u32[]{:S(2)}, u32[]{:S(2)}) %collective-permute-start.11) | collective-permute-done | bytes 40992 | tf_op jit(solution)/shard_map/ppermute | solution.py:357
  44.9 3.3 %collective-permute-start.14 = (f32[80,128]{1,0:T(8,128)S(1)}, f32[80,128]{1,0:T(8,128)S(1)}, u32[]{:S(2)}, u32[]{:S(2)}) collective-permute-start(f32[80,128]{1,0:T(8,128)S(1)} %add_add_fusion), channel_id=1, source_target_pairs={{0,224},{1,225},{2,226},{3,227},{4,228},{5,229},{6,230},{7,231},{8... | collective-permute-start | bytes 122888 | tf_op jit(solution)/shard_map/ppermute | solution.py:357
  48.2 3.8 %collective-permute-done.14 = f32[80,128]{1,0:T(8,128)S(1)} collective-permute-done((f32[80,128]{1,0:T(8,128)S(1)}, f32[80,128]{1,0:T(8,128)S(1)}, u32[]{:S(2)}, u32[]{:S(2)}) %collective-permute-start.14) | collective-permute-done | bytes 40992 | tf_op jit(solution)/shard_map/ppermute | solution.py:357
  52.0 8.5 %finish.1 = (f32[128,64,256]{2,1,0:T(8,128)}, f32[128,128]{1,0:T(8,128)}) custom-call(f32[80,128]{1,0:T(8,128)S(1)} %add.43.refs_0_, bf16[256,16384]{1,0:T(8,128)(2,1)S(1)} %get-tuple-element.19.refs_1_), custom_call_target="tpu_custom_call" | custom-call | tf_op jit(solution)/shard_map/finish/pallas_call | solution.py:334
  (5 shorter events, 0.1 us)
Async XLA Ops:
  3.6 7.8 %collective-permute-start = (f32[40,256]{1,0:T(8,128)S(1)}, f32[40,256]{1,0:T(8,128)S(1)}, u32[]{:S(2)}, u32[]{:S(2)}) collective-permute-start(f32[40,256]{1,0:T(8,128)S(1)} %get-tuple-element.14), channel_id=1, source_target_pairs={{0,8},{8,0},{16,24},{24,16},{32,40},{40,32},{48,56},{56,48},{64,72... | collective-permute-start | bytes 122888 | tf_op jit(solution)/shard_map/ppermute | solution.py:377
  5.1 6.3 %collective-permute-start.1 = (f32[40,256]{1,0:T(8,128)S(1)}, f32[40,256]{1,0:T(8,128)S(1)}, u32[]{:S(2)}, u32[]{:S(2)}) collective-permute-start(f32[40,256]{1,0:T(8,128)S(1)} %get-tuple-element.15), channel_id=1, source_target_pairs={{0,248},{8,16},{16,8},{24,32},{32,24},{40,48},{48,40},{56,64},{64,... | collective-permute-start | bytes 122888 | tf_op jit(solution)/shard_map/ppermute | solution.py:377
  6.8 3.1 %collective-permute-start.2 = (f32[40,128]{1,0:T(8,128)S(1)}, f32[40,128]{1,0:T(8,128)S(1)}, u32[]{:S(2)}, u32[]{:S(2)}) collective-permute-start(f32[40,128]{1,0:T(8,128)S(1)} %get-tuple-element.16), channel_id=1, source_target_pairs={{0,1},{1,0},{2,3},{3,2},{4,5},{5,4},{6,7},{7,6},{8,9},{9,8},{10,11... | collective-permute-start | bytes 61448 | tf_op jit(solution)/shard_map/ppermute | solution.py:377
  6.8 4.6 %collective-permute-start.3 = (f32[40,128]{1,0:T(8,128)S(1)}, f32[40,128]{1,0:T(8,128)S(1)}, u32[]{:S(2)}, u32[]{:S(2)}) collective-permute-start(f32[40,128]{1,0:T(8,128)S(1)} %get-tuple-element.17), channel_id=1, source_target_pairs={{0,7},{1,2},{2,1},{3,4},{4,3},{5,6},{6,5},{7,0},{8,15},{9,10},{10,... | collective-permute-start | bytes 61448 | tf_op jit(solution)/shard_map/ppermute | solution.py:377
  16.1 1.3 %collective-permute-start.4 = (f32[80,128]{1,0:T(8,128)S(1)}, f32[80,128]{1,0:T(8,128)S(1)}, u32[]{:S(2)}, u32[]{:S(2)}) collective-permute-start(f32[80,128]{1,0:T(8,128)S(1)} %get-tuple-element.18), channel_id=1, source_target_pairs={{0,1},{1,0},{2,3},{3,2},{4,5},{5,4},{6,7},{7,6},{8,9},{9,8},{10,11... | collective-permute-start | bytes 122888 | tf_op jit(solution)/shard_map/ppermute | solution.py:357
  17.5 5.2 %collective-permute-start.7 = (f32[80,128]{1,0:T(8,128)S(1)}, f32[80,128]{1,0:T(8,128)S(1)}, u32[]{:S(2)}, u32[]{:S(2)}) collective-permute-start(f32[80,128]{1,0:T(8,128)S(1)} %add.33), channel_id=1, source_target_pairs={{0,24},{1,7},{2,26},{3,5},{4,28},{5,3},{6,30},{7,1},{8,16},{9,15},... | collective-permute-start | bytes 122888 | tf_op jit(solution)/shard_map/ppermute | solution.py:357
  20.4 5.5 %collective-permute-start.6 = (f32[80,128]{1,0:T(8,128)S(1)}, f32[80,128]{1,0:T(8,128)S(1)}, u32[]{:S(2)}, u32[]{:S(2)}) collective-permute-start(f32[80,128]{1,0:T(8,128)S(1)} %add.33), channel_id=1, source_target_pairs={{0,16},{1,5},{2,18},{3,7},{4,20},{5,1},{6,22},{7,3},{8,24},{9,13},... | collective-permute-start | bytes 122888 | tf_op jit(solution)/shard_map/ppermute | solution.py:357
  20.6 5.3 %collective-permute-start.5 = (f32[80,128]{1,0:T(8,128)S(1)}, f32[80,128]{1,0:T(8,128)S(1)}, u32[]{:S(2)}, u32[]{:S(2)}) collective-permute-start(f32[80,128]{1,0:T(8,128)S(1)} %add.33), channel_id=1, source_target_pairs={{0,8},{1,3},{2,10},{3,1},{4,12},{5,7},{6,14},{7,5},{8,0},{9,11},{1... | collective-permute-start | bytes 122888 | tf_op jit(solution)/shard_map/ppermute | solution.py:357
  25.9 5.3 %collective-permute-start.10 = (f32[80,128]{1,0:T(8,128)S(1)}, f32[80,128]{1,0:T(8,128)S(1)}, u32[]{:S(2)}, u32[]{:S(2)}) collective-permute-start(f32[80,128]{1,0:T(8,128)S(1)} %add_add_fusion.2), channel_id=1, source_target_pairs={{0,6},{1,25},{2,4},{3,27},{4,2},{5,29},{6,0},{7,31},{8,14},{9,17},... | collective-permute-start | bytes 122888 | tf_op jit(solution)/shard_map/ppermute | solution.py:357
  29.0 5.5 %collective-permute-start.9 = (f32[80,128]{1,0:T(8,128)S(1)}, f32[80,128]{1,0:T(8,128)S(1)}, u32[]{:S(2)}, u32[]{:S(2)}) collective-permute-start(f32[80,128]{1,0:T(8,128)S(1)} %add_add_fusion.2), channel_id=1, source_target_pairs={{0,4},{1,17},{2,6},{3,19},{4,0},{5,21},{6,2},{7,23},{8,12},{9,25},... | collective-permute-start | bytes 122888 | tf_op jit(solution)/shard_map/ppermute | solution.py:357
  29.0 5.5 %collective-permute-start.8 = (f32[80,128]{1,0:T(8,128)S(1)}, f32[80,128]{1,0:T(8,128)S(1)}, u32[]{:S(2)}, u32[]{:S(2)}) collective-permute-start(f32[80,128]{1,0:T(8,128)S(1)} %add_add_fusion.2), channel_id=1, source_target_pairs={{0,2},{1,9},{2,0},{3,11},{4,6},{5,13},{6,4},{7,15},{8,10},{9,1},{1... | collective-permute-start | bytes 122888 | tf_op jit(solution)/shard_map/ppermute | solution.py:357
  34.5 6.4 %collective-permute-start.13 = (f32[80,128]{1,0:T(8,128)S(1)}, f32[80,128]{1,0:T(8,128)S(1)}, u32[]{:S(2)}, u32[]{:S(2)}) collective-permute-start(f32[80,128]{1,0:T(8,128)S(1)} %add_add_fusion.1), channel_id=1, source_target_pairs={{0,96},{1,97},{2,98},{3,99},{4,100},{5,101},{6,102},{7,103},{8,104... | collective-permute-start | bytes 122888 | tf_op jit(solution)/shard_map/ppermute | solution.py:357
  36.5 6.8 %collective-permute-start.12 = (f32[80,128]{1,0:T(8,128)S(1)}, f32[80,128]{1,0:T(8,128)S(1)}, u32[]{:S(2)}, u32[]{:S(2)}) collective-permute-start(f32[80,128]{1,0:T(8,128)S(1)} %add_add_fusion.1), channel_id=1, source_target_pairs={{0,64},{1,65},{2,66},{3,67},{4,68},{5,69},{6,70},{7,71},{8,72},{9,... | collective-permute-start | bytes 122888 | tf_op jit(solution)/shard_map/ppermute | solution.py:357
  40.9 4.0 %collective-permute-start.11 = (f32[80,128]{1,0:T(8,128)S(1)}, f32[80,128]{1,0:T(8,128)S(1)}, u32[]{:S(2)}, u32[]{:S(2)}) collective-permute-start(f32[80,128]{1,0:T(8,128)S(1)} %add_add_fusion.1), channel_id=1, source_target_pairs={{0,32},{1,33},{2,34},{3,35},{4,36},{5,37},{6,38},{7,39},{8,40},{9,... | collective-permute-start | bytes 122888 | tf_op jit(solution)/shard_map/ppermute | solution.py:357
  44.9 7.1 %collective-permute-start.14 = (f32[80,128]{1,0:T(8,128)S(1)}, f32[80,128]{1,0:T(8,128)S(1)}, u32[]{:S(2)}, u32[]{:S(2)}) collective-permute-start(f32[80,128]{1,0:T(8,128)S(1)} %add_add_fusion), channel_id=1, source_target_pairs={{0,224},{1,225},{2,226},{3,227},{4,228},{5,229},{6,230},{7,231},{8... | collective-permute-start | bytes 122888 | tf_op jit(solution)/shard_map/ppermute | solution.py:357

commit v5 on v4

--- a/solution.py
+++ b/solution.py
@@ -45,7 +45,7 @@
         if n == 0:
             for t in range(sides):
                 arrive(g, t).wait()
-        here = lane == i
+        here, one_before = lane == i, lane == (i - 1) % 128
         parts = [buf[g, t, pl.ds(n, K, stride=8), :] for t in range(sides)]
         for t in range(sides):
             rows_ref[K * i : K * i + K, 128 * t : 128 * t + 128] = parts[t]
@@ -59,8 +59,10 @@
                 first, last = conduct[:, :128], conduct[:, cols - 128 :]
             else:
                 first, last = parts[0][8 * b : 8 * b + 8], parts[-1][8 * b : 8 * b + 8]
-            left[b] = jnp.where(here, pltpu.roll(first, i, 1) if i else first, left[b])
-            right[b] = jnp.where(here, pltpu.roll(last, (i + 1) % 128, 1), right[b])
+            both = jnp.where(lane < 64, first, last)
+            turned = pltpu.roll(both, i, 1) if i else both
+            left[b] = jnp.where(here, turned, left[b])
+            right[b] = jnp.where(one_before, turned, right[b])
     for b in range(K // 8 + 1):
         y1_ref[8 * b : 8 * b + 8, :] = jnp.where(even_y, right[b], left[b])
         y2_ref[8 * b : 8 * b + 8, :] = jnp.where(even_y, left[b], right[b])
@@ -149,7 +151,7 @@
                 u_next, k_next = u_after, k_after
             u_t, k_t = tiles(u_now), tiles(k_now)
             flux = [spread(a) * (b - c) for a, b, c in zip(tiles(0.5 * (k_now + k_next)), u_t, tiles(u_next))]
-            left = pltpu.roll(lf_ref[...], 128 - i, 1)
+            left = pltpu.roll(lf_ref[...], (129 - i) % 128, 1)
             right = pltpu.roll(rt_ref[...], 127 - i, 1)
             k_right = shifted_left(k_t, right[K : K + 1], lane8[:1])
             u_right = shifted_left(u_t, right[:K], lane)
@@ -221,6 +223,19 @@
     a = [gram[NB * q : NB * q + NB] for q in range(blocks)]
     e = [jnp.where(lane == sub + NB * q, 1.0, 0.0).astype(F32) for q in range(blocks)]
     upper, inverse = [], []
+
+    def stacked(parts):
+        out = parts[0]
+        for k in range(1, NB):
+            out = jnp.where(sub == k, parts[k], out)
+        return out
+
+    def three(value):
+        first = value.astype(BF16).astype(F32)
+        rest = value - first
+        second = rest.astype(BF16).astype(F32)
+        return first, second, rest - second
+
     for p in range(blocks):
         col = lambda m, j: jnp.broadcast_to(m[:, NB * p + j : NB * p + j + 1], shape)
         row = lambda m, j: jnp.broadcast_to(m[j : j + 1, :], shape)
@@ -261,19 +276,30 @@
 
         ra = combine([row(a[p], j) for j in range(NB)])
         re = combine([row(e[p], j) for j in range(NB)])
-        ua, ue = ra[0], re[0]
-        for k in range(1, NB):
-            ua = jnp.where(sub == k, ra[k], ua)
-            ue = jnp.where(sub == k, re[k], ue)
+        ua, ue = stacked(ra), stacked(re)
         upper.append(jnp.where(lane >= sub + NB * p, ua, 0.0))
         inverse.append(ue)
         wa, we = solved(ra), solved(re)
-        for q in range(p + 1, blocks):
+        near = min(p + 1 + 1, blocks)
+        for q in range(p + 1, near):
             c = [col(a[q], j) for j in range(NB)]
             sa, se = c[0] * wa[0], c[0] * we[0]
             for k in range(1, NB):
                 sa, se = sa + c[k] * wa[k], se + c[k] * we[k]
             a[q], e[q] = a[q] - sa, e[q] - se
+        if near < blocks:
+            w = jnp.concatenate([stacked(wa), stacked(we)], 1)
+            p0, p1, p2 = three(a[p])
+            w0, w1, w2 = three(w)
+            delta = lax.dot_general(
+                jnp.concatenate([p0, p0, p1, p1, p0, p2], 0).astype(BF16),
+                jnp.concatenate([w0, w1, w0, w1, w2, w0], 0).astype(BF16),
+                (((0,), (0,)), ((), ())),
+                preferred_element_type=F32,
+            )
+            for q in range(near, blocks):
+                a[q] = a[q] - delta[NB * q : NB * q + NB, :C]
+                e[q] = e[q] - delta[NB * q : NB * q + NB, C:]
         after_panel(p, inverse)
     return upper, inverse
 

time: 60.8 us -> 59.8 us (0.984)
  Pallas kernels: 16.1 us -> 15.1 us
    pallas_call x1, Pallas kernels: 8.46 us -> 7.77 us  [finish(): pl.pallas_call(lambda *refs: finish_kernel(rows, cols, *refs), name='fini...]
where the time goes in v5:
time: 59.8 us; the launch traced here: 59.6 us
  starting transfers between devices  24.4 us (41%)
  waiting for transfers between devices  19.3 us (32%)
  Pallas kernels  15.1 us (25%)
  between operations  0.83 us (1%)
    ppermute x11, starting transfers between devices, exchanged(): return lax.ppermute(value, ('gx', 'gy'), pairs)  18 us
    ppermute x11, waiting for transfers between devices, exchanged(): return lax.ppermute(value, ('gx', 'gy'), pairs)  17.8 us
    pallas_call x1, Pallas kernels, finish(): pl.pallas_call(lambda *refs: finish_kernel(rows, cols, *refs), name='fini...  7.77 us
    ppermute x4, starting transfers between devices, swap(): lax.ppermute(value, axis, [(i, (i + 1 if (i % 2 == 0) == first else i - 1...  6.35 us
    pallas_call x1, Pallas kernels, columns_and_gram(): pl.pallas_call(lambda *refs: gram_kernel(rows, cols, places, scale, *refs...  4.74 us
    pallas_call x1, Pallas kernels, edges(): pl.pallas_call(lambda *refs: edges_kernel(rows, cols, *refs), name='edges...  2.64 us
    ppermute x4, waiting for transfers between devices, swap(): lax.ppermute(value, axis, [(i, (i + 1 if (i % 2 == 0) == first else i - 1...  1.49 us
  transfers between devices with their start and end apart: 15, of which 9 were waited for; matrix products, arithmetic and copies ran while one was open for 0% of the time, Pallas kernels for 0%

profile of v5, /device:TPU:32, one launch (start us, length us, event | category | flops | bytes accessed | tf_op | source)
XLA Modules:
  0.0 59.6 jit_solution(9245546592671140910)
XLA Ops:
  0.6 2.6 %edges.1 = (f32[40,256]{1,0:T(8,128)S(1)}, f32[40,256]{1,0:T(8,128)S(1)}, f32[40,128]{1,0:T(8,128)S(1)}, f32[40,128]{1,0:T(8,128)S(1)}, f32[2048,256]{1,0:T(8,12...) custom-call(f32[32,64,256]{2,1,0:T(8,128)} %refs_0_.1, f32[64,256]{1,0:T(8,128)} %refs_1_.1, f32[64,256]{1,0:T(8,128)} %refs_2_.1), custom_call_target="tpu_custom_call" | custom-call | tf_op jit(solution)/shard_map/edges/pallas_call | solution.py:79
  3.3 1.6 %collective-permute-start = (f32[40,256]{1,0:T(8,128)S(1)}, f32[40,256]{1,0:T(8,128)S(1)}, u32[]{:S(2)}, u32[]{:S(2)}) collective-permute-start(f32[40,256]{1,0:T(8,128)S(1)} %get-tuple-element.14), channel_id=1, source_target_pairs={{0,8},{8,0},{16,24},{24,16},{32,40},{40,32},{48,56},{56,48},{64,72... | collective-permute-start | bytes 122888 | tf_op jit(solution)/shard_map/ppermute | solution.py:403
  4.9 1.6 %collective-permute-start.1 = (f32[40,256]{1,0:T(8,128)S(1)}, f32[40,256]{1,0:T(8,128)S(1)}, u32[]{:S(2)}, u32[]{:S(2)}) collective-permute-start(f32[40,256]{1,0:T(8,128)S(1)} %get-tuple-element.15), channel_id=1, source_target_pairs={{0,248},{8,16},{16,8},{24,32},{32,24},{40,48},{48,40},{56,64},{64,... | collective-permute-start | bytes 122888 | tf_op jit(solution)/shard_map/ppermute | solution.py:403
  6.5 0.0 collective-permute-start.2
  6.5 3.1 %collective-permute-start.3 = (f32[40,128]{1,0:T(8,128)S(1)}, f32[40,128]{1,0:T(8,128)S(1)}, u32[]{:S(2)}, u32[]{:S(2)}) collective-permute-start(f32[40,128]{1,0:T(8,128)S(1)} %get-tuple-element.17), channel_id=1, source_target_pairs={{0,7},{1,2},{2,1},{3,4},{4,3},{5,6},{6,5},{7,0},{8,15},{9,10},{10,... | collective-permute-start | bytes 61448 | tf_op jit(solution)/shard_map/ppermute | solution.py:403
  9.6 0.0 collective-permute-done.2.refs_5_
  9.6 1.5 %collective-permute-done.3.refs_6_ = f32[40,128]{1,0:T(8,128)S(1)} collective-permute-done((f32[40,128]{1,0:T(8,128)S(1)}, f32[40,128]{1,0:T(8,128)S(1)}, u32[]{:S(2)}, u32[]{:S(2)}) %collective-permute-start.3) | collective-permute-done | bytes 20512 | tf_op jit(solution)/shard_map/ppermute | solution.py:403
  11.1 0.0 collective-permute-done.refs_3_
  11.1 0.0 collective-permute-done.1.refs_4_
  11.1 4.7 %gram.1 = (f32[80,128]{1,0:T(8,128)S(1)}, bf16[256,16384]{1,0:T(8,128)(2,1)S(1)}) custom-call(f32[2048,256]{1,0:T(8,128)S(1)} %get-tuple-element.11.refs_0_, f32[64,256]{1,0:T(8,128)S(1)} %get-tuple-element.12.refs_1_, f32[64,256]{1,0:T(8,128)S(1)} %get-tuple-element.13.refs_2_, f32[40,256]{1,0:T(8,128)S(1)} %collective-permute-done.refs_3_, ...), custom_call_target="tpu_custom_call" | custom-call | tf_op jit(solution)/shard_map/gram/pallas_call | solution.py:207
  15.8 0.1 collective-permute-start.4
  15.9 1.2 %collective-permute-done.4 = f32[80,128]{1,0:T(8,128)S(1)} collective-permute-done((f32[80,128]{1,0:T(8,128)S(1)}, f32[80,128]{1,0:T(8,128)S(1)}, u32[]{:S(2)}, u32[]{:S(2)}) %collective-permute-start.4) | collective-permute-done | bytes 40992 | tf_op jit(solution)/shard_map/ppermute | solution.py:383
  17.2 3.0 %collective-permute-start.7 = (f32[80,128]{1,0:T(8,128)S(1)}, f32[80,128]{1,0:T(8,128)S(1)}, u32[]{:S(2)}, u32[]{:S(2)}) collective-permute-start(f32[80,128]{1,0:T(8,128)S(1)} %add.33), channel_id=1, source_target_pairs={{0,24},{1,7},{2,26},{3,5},{4,28},{5,3},{6,30},{7,1},{8,16},{9,15},... | collective-permute-start | bytes 122888 | tf_op jit(solution)/shard_map/ppermute | solution.py:383
  20.1 0.2 collective-permute-start.6
  20.3 1.0 %collective-permute-start.5 = (f32[80,128]{1,0:T(8,128)S(1)}, f32[80,128]{1,0:T(8,128)S(1)}, u32[]{:S(2)}, u32[]{:S(2)}) collective-permute-start(f32[80,128]{1,0:T(8,128)S(1)} %add.33), channel_id=1, source_target_pairs={{0,8},{1,3},{2,10},{3,1},{4,12},{5,7},{6,14},{7,5},{8,0},{9,11},{1... | collective-permute-start | bytes 122888 | tf_op jit(solution)/shard_map/ppermute | solution.py:383
  21.3 1.1 %collective-permute-done.7 = f32[80,128]{1,0:T(8,128)S(1)} collective-permute-done((f32[80,128]{1,0:T(8,128)S(1)}, f32[80,128]{1,0:T(8,128)S(1)}, u32[]{:S(2)}, u32[]{:S(2)}) %collective-permute-start.7) | collective-permute-done | bytes 40992 | tf_op jit(solution)/shard_map/ppermute | solution.py:383
  22.4 3.2 %collective-permute-done.6 = f32[80,128]{1,0:T(8,128)S(1)} collective-permute-done((f32[80,128]{1,0:T(8,128)S(1)}, f32[80,128]{1,0:T(8,128)S(1)}, u32[]{:S(2)}, u32[]{:S(2)}) %collective-permute-start.6) | collective-permute-done | bytes 40992 | tf_op jit(solution)/shard_map/ppermute | solution.py:383
  25.6 0.0 collective-permute-done.5
  25.6 3.1 %collective-permute-start.10 = (f32[80,128]{1,0:T(8,128)S(1)}, f32[80,128]{1,0:T(8,128)S(1)}, u32[]{:S(2)}, u32[]{:S(2)}) collective-permute-start(f32[80,128]{1,0:T(8,128)S(1)} %add_add_fusion.2), channel_id=1, source_target_pairs={{0,6},{1,25},{2,4},{3,27},{4,2},{5,29},{6,0},{7,31},{8,14},{9,17},... | collective-permute-start | bytes 122888 | tf_op jit(solution)/shard_map/ppermute | solution.py:383
  28.7 0.0 collective-permute-start.9
  28.7 1.1 %collective-permute-start.8 = (f32[80,128]{1,0:T(8,128)S(1)}, f32[80,128]{1,0:T(8,128)S(1)}, u32[]{:S(2)}, u32[]{:S(2)}) collective-permute-start(f32[80,128]{1,0:T(8,128)S(1)} %add_add_fusion.2), channel_id=1, source_target_pairs={{0,2},{1,9},{2,0},{3,11},{4,6},{5,13},{6,4},{7,15},{8,10},{9,1},{1... | collective-permute-start | bytes 122888 | tf_op jit(solution)/shard_map/ppermute | solution.py:383
  29.8 1.1 %collective-permute-done.10 = f32[80,128]{1,0:T(8,128)S(1)} collective-permute-done((f32[80,128]{1,0:T(8,128)S(1)}, f32[80,128]{1,0:T(8,128)S(1)}, u32[]{:S(2)}, u32[]{:S(2)}) %collective-permute-start.10) | collective-permute-done | bytes 40992 | tf_op jit(solution)/shard_map/ppermute | solution.py:383
  30.9 3.3 %collective-permute-done.9 = f32[80,128]{1,0:T(8,128)S(1)} collective-permute-done((f32[80,128]{1,0:T(8,128)S(1)}, f32[80,128]{1,0:T(8,128)S(1)}, u32[]{:S(2)}, u32[]{:S(2)}) %collective-permute-start.9) | collective-permute-done | bytes 40992 | tf_op jit(solution)/shard_map/ppermute | solution.py:383
  34.2 0.0 collective-permute-done.8
  34.2 2.0 %collective-permute-start.13 = (f32[80,128]{1,0:T(8,128)S(1)}, f32[80,128]{1,0:T(8,128)S(1)}, u32[]{:S(2)}, u32[]{:S(2)}) collective-permute-start(f32[80,128]{1,0:T(8,128)S(1)} %add_add_fusion.1), channel_id=1, source_target_pairs={{0,96},{1,97},{2,98},{3,99},{4,100},{5,101},{6,102},{7,103},{8,104... | collective-permute-start | bytes 122888 | tf_op jit(solution)/shard_map/ppermute | solution.py:383
  36.2 4.3 %collective-permute-start.12 = (f32[80,128]{1,0:T(8,128)S(1)}, f32[80,128]{1,0:T(8,128)S(1)}, u32[]{:S(2)}, u32[]{:S(2)}) collective-permute-start(f32[80,128]{1,0:T(8,128)S(1)} %add_add_fusion.1), channel_id=1, source_target_pairs={{0,64},{1,65},{2,66},{3,67},{4,68},{5,69},{6,70},{7,71},{8,72},{9,... | collective-permute-start | bytes 122888 | tf_op jit(solution)/shard_map/ppermute | solution.py:383
  40.6 0.0 collective-permute-start.11
  40.6 0.0 collective-permute-done.13
  40.6 2.4 %collective-permute-done.12 = f32[80,128]{1,0:T(8,128)S(1)} collective-permute-done((f32[80,128]{1,0:T(8,128)S(1)}, f32[80,128]{1,0:T(8,128)S(1)}, u32[]{:S(2)}, u32[]{:S(2)}) %collective-permute-start.12) | collective-permute-done | bytes 40992 | tf_op jit(solution)/shard_map/ppermute | solution.py:383
  43.0 1.6 %collective-permute-done.11 = f32[80,128]{1,0:T(8,128)S(1)} collective-permute-done((f32[80,128]{1,0:T(8,128)S(1)}, f32[80,128]{1,0:T(8,128)S(1)}, u32[]{:S(2)}, u32[]{:S(2)}) %collective-permute-start.11) | collective-permute-done | bytes 40992 | tf_op jit(solution)/shard_map/ppermute | solution.py:383
  44.6 3.3 %collective-permute-start.14 = (f32[80,128]{1,0:T(8,128)S(1)}, f32[80,128]{1,0:T(8,128)S(1)}, u32[]{:S(2)}, u32[]{:S(2)}) collective-permute-start(f32[80,128]{1,0:T(8,128)S(1)} %add_add_fusion), channel_id=1, source_target_pairs={{0,224},{1,225},{2,226},{3,227},{4,228},{5,229},{6,230},{7,231},{8... | collective-permute-start | bytes 122888 | tf_op jit(solution)/shard_map/ppermute | solution.py:383
  47.9 3.8 %collective-permute-done.14 = f32[80,128]{1,0:T(8,128)S(1)} collective-permute-done((f32[80,128]{1,0:T(8,128)S(1)}, f32[80,128]{1,0:T(8,128)S(1)}, u32[]{:S(2)}, u32[]{:S(2)}) %collective-permute-start.14) | collective-permute-done | bytes 40992 | tf_op jit(solution)/shard_map/ppermute | solution.py:383
  51.7 7.8 %finish.1 = (f32[128,64,256]{2,1,0:T(8,128)}, f32[128,128]{1,0:T(8,128)}) custom-call(f32[80,128]{1,0:T(8,128)S(1)} %add.43.refs_0_, bf16[256,16384]{1,0:T(8,128)(2,1)S(1)} %get-tuple-element.19.refs_1_), custom_call_target="tpu_custom_call" | custom-call | tf_op jit(solution)/shard_map/finish/pallas_call | solution.py:360
  (5 shorter events, 0.1 us)
Async XLA Ops:
  3.3 7.8 %collective-permute-start = (f32[40,256]{1,0:T(8,128)S(1)}, f32[40,256]{1,0:T(8,128)S(1)}, u32[]{:S(2)}, u32[]{:S(2)}) collective-permute-start(f32[40,256]{1,0:T(8,128)S(1)} %get-tuple-element.14), channel_id=1, source_target_pairs={{0,8},{8,0},{16,24},{24,16},{32,40},{40,32},{48,56},{56,48},{64,72... | collective-permute-start | bytes 122888 | tf_op jit(solution)/shard_map/ppermute | solution.py:403
  4.9 6.3 %collective-permute-start.1 = (f32[40,256]{1,0:T(8,128)S(1)}, f32[40,256]{1,0:T(8,128)S(1)}, u32[]{:S(2)}, u32[]{:S(2)}) collective-permute-start(f32[40,256]{1,0:T(8,128)S(1)} %get-tuple-element.15), channel_id=1, source_target_pairs={{0,248},{8,16},{16,8},{24,32},{32,24},{40,48},{48,40},{56,64},{64,... | collective-permute-start | bytes 122888 | tf_op jit(solution)/shard_map/ppermute | solution.py:403
  6.5 3.1 %collective-permute-start.2 = (f32[40,128]{1,0:T(8,128)S(1)}, f32[40,128]{1,0:T(8,128)S(1)}, u32[]{:S(2)}, u32[]{:S(2)}) collective-permute-start(f32[40,128]{1,0:T(8,128)S(1)} %get-tuple-element.16), channel_id=1, source_target_pairs={{0,1},{1,0},{2,3},{3,2},{4,5},{5,4},{6,7},{7,6},{8,9},{9,8},{10,11... | collective-permute-start | bytes 61448 | tf_op jit(solution)/shard_map/ppermute | solution.py:403
  6.5 4.6 %collective-permute-start.3 = (f32[40,128]{1,0:T(8,128)S(1)}, f32[40,128]{1,0:T(8,128)S(1)}, u32[]{:S(2)}, u32[]{:S(2)}) collective-permute-start(f32[40,128]{1,0:T(8,128)S(1)} %get-tuple-element.17), channel_id=1, source_target_pairs={{0,7},{1,2},{2,1},{3,4},{4,3},{5,6},{6,5},{7,0},{8,15},{9,10},{10,... | collective-permute-start | bytes 61448 | tf_op jit(solution)/shard_map/ppermute | solution.py:403
  15.8 1.3 %collective-permute-start.4 = (f32[80,128]{1,0:T(8,128)S(1)}, f32[80,128]{1,0:T(8,128)S(1)}, u32[]{:S(2)}, u32[]{:S(2)}) collective-permute-start(f32[80,128]{1,0:T(8,128)S(1)} %get-tuple-element.18), channel_id=1, source_target_pairs={{0,1},{1,0},{2,3},{3,2},{4,5},{5,4},{6,7},{7,6},{8,9},{9,8},{10,11... | collective-permute-start | bytes 122888 | tf_op jit(solution)/shard_map/ppermute | solution.py:383
  17.2 5.2 %collective-permute-start.7 = (f32[80,128]{1,0:T(8,128)S(1)}, f32[80,128]{1,0:T(8,128)S(1)}, u32[]{:S(2)}, u32[]{:S(2)}) collective-permute-start(f32[80,128]{1,0:T(8,128)S(1)} %add.33), channel_id=1, source_target_pairs={{0,24},{1,7},{2,26},{3,5},{4,28},{5,3},{6,30},{7,1},{8,16},{9,15},... | collective-permute-start | bytes 122888 | tf_op jit(solution)/shard_map/ppermute | solution.py:383
  20.1 5.5 %collective-permute-start.6 = (f32[80,128]{1,0:T(8,128)S(1)}, f32[80,128]{1,0:T(8,128)S(1)}, u32[]{:S(2)}, u32[]{:S(2)}) collective-permute-start(f32[80,128]{1,0:T(8,128)S(1)} %add.33), channel_id=1, source_target_pairs={{0,16},{1,5},{2,18},{3,7},{4,20},{5,1},{6,22},{7,3},{8,24},{9,13},... | collective-permute-start | bytes 122888 | tf_op jit(solution)/shard_map/ppermute | solution.py:383
  20.3 5.3 %collective-permute-start.5 = (f32[80,128]{1,0:T(8,128)S(1)}, f32[80,128]{1,0:T(8,128)S(1)}, u32[]{:S(2)}, u32[]{:S(2)}) collective-permute-start(f32[80,128]{1,0:T(8,128)S(1)} %add.33), channel_id=1, source_target_pairs={{0,8},{1,3},{2,10},{3,1},{4,12},{5,7},{6,14},{7,5},{8,0},{9,11},{1... | collective-permute-start | bytes 122888 | tf_op jit(solution)/shard_map/ppermute | solution.py:383
  25.6 5.3 %collective-permute-start.10 = (f32[80,128]{1,0:T(8,128)S(1)}, f32[80,128]{1,0:T(8,128)S(1)}, u32[]{:S(2)}, u32[]{:S(2)}) collective-permute-start(f32[80,128]{1,0:T(8,128)S(1)} %add_add_fusion.2), channel_id=1, source_target_pairs={{0,6},{1,25},{2,4},{3,27},{4,2},{5,29},{6,0},{7,31},{8,14},{9,17},... | collective-permute-start | bytes 122888 | tf_op jit(solution)/shard_map/ppermute | solution.py:383
  28.7 5.5 %collective-permute-start.9 = (f32[80,128]{1,0:T(8,128)S(1)}, f32[80,128]{1,0:T(8,128)S(1)}, u32[]{:S(2)}, u32[]{:S(2)}) collective-permute-start(f32[80,128]{1,0:T(8,128)S(1)} %add_add_fusion.2), channel_id=1, source_target_pairs={{0,4},{1,17},{2,6},{3,19},{4,0},{5,21},{6,2},{7,23},{8,12},{9,25},... | collective-permute-start | bytes 122888 | tf_op jit(solution)/shard_map/ppermute | solution.py:383
  28.7 5.5 %collective-permute-start.8 = (f32[80,128]{1,0:T(8,128)S(1)}, f32[80,128]{1,0:T(8,128)S(1)}, u32[]{:S(2)}, u32[]{:S(2)}) collective-permute-start(f32[80,128]{1,0:T(8,128)S(1)} %add_add_fusion.2), channel_id=1, source_target_pairs={{0,2},{1,9},{2,0},{3,11},{4,6},{5,13},{6,4},{7,15},{8,10},{9,1},{1... | collective-permute-start | bytes 122888 | tf_op jit(solution)/shard_map/ppermute | solution.py:383
  34.2 6.4 %collective-permute-start.13 = (f32[80,128]{1,0:T(8,128)S(1)}, f32[80,128]{1,0:T(8,128)S(1)}, u32[]{:S(2)}, u32[]{:S(2)}) collective-permute-start(f32[80,128]{1,0:T(8,128)S(1)} %add_add_fusion.1), channel_id=1, source_target_pairs={{0,96},{1,97},{2,98},{3,99},{4,100},{5,101},{6,102},{7,103},{8,104... | collective-permute-start | bytes 122888 | tf_op jit(solution)/shard_map/ppermute | solution.py:383
  36.2 6.8 %collective-permute-start.12 = (f32[80,128]{1,0:T(8,128)S(1)}, f32[80,128]{1,0:T(8,128)S(1)}, u32[]{:S(2)}, u32[]{:S(2)}) collective-permute-start(f32[80,128]{1,0:T(8,128)S(1)} %add_add_fusion.1), channel_id=1, source_target_pairs={{0,64},{1,65},{2,66},{3,67},{4,68},{5,69},{6,70},{7,71},{8,72},{9,... | collective-permute-start | bytes 122888 | tf_op jit(solution)/shard_map/ppermute | solution.py:383
  40.6 4.0 %collective-permute-start.11 = (f32[80,128]{1,0:T(8,128)S(1)}, f32[80,128]{1,0:T(8,128)S(1)}, u32[]{:S(2)}, u32[]{:S(2)}) collective-permute-start(f32[80,128]{1,0:T(8,128)S(1)} %add_add_fusion.1), channel_id=1, source_target_pairs={{0,32},{1,33},{2,34},{3,35},{4,36},{5,37},{6,38},{7,39},{8,40},{9,... | collective-permute-start | bytes 122888 | tf_op jit(solution)/shard_map/ppermute | solution.py:383
  44.6 7.1 %collective-permute-start.14 = (f32[80,128]{1,0:T(8,128)S(1)}, f32[80,128]{1,0:T(8,128)S(1)}, u32[]{:S(2)}, u32[]{:S(2)}) collective-permute-start(f32[80,128]{1,0:T(8,128)S(1)} %add_add_fusion), channel_id=1, source_target_pairs={{0,224},{1,225},{2,226},{3,227},{4,228},{5,229},{6,230},{7,231},{8... | collective-permute-start | bytes 122888 | tf_op jit(solution)/shard_map/ppermute | solution.py:383
